TPU v7x, 32 devices: a whole 2x2x4 slice. The times are simulated.
32 devices in a mesh: blk: 16 (over z, y, core), grp: 2 (over x).
Axes of the slice: x: 2, y: 2, z: 4, core: 2. Of those that a mesh axis runs over, the one named last changes fastest.
Arguments:
- images: float32 [4096, 768], P(('blk', 'grp')), may hold values from -0.24 to 0.24
- texts: float32 [4096, 768], P(('blk', 'grp')), may hold values from -0.24 to 0.24
- log_temp: float32 [1], replicated, may hold values from 2.3 to 3
- bias: float32 [1], replicated, may hold values from -3 to -1
- row_weight: float32 [4096], P(('blk', 'grp')), may hold values from 0.5 to 2
Outputs:
- row_loss: float32 [4096], P(('blk', 'grp'))
- grad_images: float32 [4096, 768], P(('blk', 'grp'))
- grad_texts: float32 [4096, 768], P(('blk', 'grp'))
All inputs are finite; a program needn't handle non-finite values.
Results may differ from a plain program's by a relative error of at most 0.00013.
Values sent between devices are 32-bit elements; how exact they have to be, the bound alone decides.
No kernel may reach another device: no remote copies, remote signals or barrier semaphores. Data moves between devices by JAX's collectives and lax.ppermute only.
A program may use at most 64 MiB of HBM per device.

v0:
```python
import jax
import jax.numpy as jnp
from jax import lax
from jax.sharding import PartitionSpec as P

REACH = 1


def passed_along(x, axis, by):
    length = lax.axis_size(axis)
    return lax.ppermute(x, axis, [(i, (i + by) % length) for i in range(length)])


def normed(values):
    scale = lax.rsqrt(jnp.sum(values * values, axis=1, keepdims=True) + 1e-06)
    return (values * scale, scale)


def unnormed(grad, unit, scale):
    return scale * (grad - unit * jnp.sum(unit * grad, axis=1, keepdims=True))


def tile_terms(left, right, temper, offset_b, weight, positive):
    logits = (
        temper * jnp.einsum("id,jd->ij", left, right, precision=lax.Precision.HIGHEST) + offset_b
    )
    labels = jnp.where(positive, 1.0, -1.0)
    losses = jax.nn.softplus(-labels * logits)
    slope = -labels * jax.nn.sigmoid(-labels * logits) * weight[:, None]
    return (jnp.sum(losses, axis=1), slope)


def shards(images, texts, log_temp, bias, row_weight):
    unit_x, scale_x = normed(images)
    unit_y, scale_y = normed(texts)
    temper = jnp.exp(log_temp[0])
    offset_b = bias[0]
    count = images.shape[0]
    members = lax.axis_size("grp")
    group = count * members
    mine = lax.axis_index("grp")
    group_x, group_w = (
        lax.all_gather(unit_x, "grp", axis=0, tiled=True),
        lax.all_gather(row_weight, "grp", axis=0, tiled=True),
    )
    window = {0: unit_y}
    current = unit_y
    step = 1
    current = passed_along(current, "blk", -1)
    window[step] = current
    current = unit_y
    step = 1
    current = passed_along(current, "blk", 1)
    window[-step] = current
    rows = lax.broadcasted_iota(jnp.int32, (group, count), 0)
    cols = lax.broadcasted_iota(jnp.int32, (group, count), 1)
    diagonal = rows == mine * count + cols
    nothing = jnp.zeros((group, count), bool)
    grad_group = jnp.zeros_like(group_x)
    group_sums = jnp.zeros((group,), jnp.float32)
    text_terms = {}
    for offset in range(-REACH, REACH + 1):
        positive = diagonal if offset == 0 else nothing
        part_sums, slope = tile_terms(group_x, window[offset], temper, offset_b, group_w, positive)
        group_sums = group_sums + part_sums
        grad_group = grad_group + temper * jnp.dot(
            slope, window[offset], precision=lax.Precision.HIGHEST
        )
        text_terms[offset] = temper * jnp.einsum(
            "ij,id->jd", slope, group_x, precision=lax.Precision.HIGHEST
        )
    step = 1
    carried = passed_along(text_terms[step], "blk", 1)
    step = 1
    returned = passed_along(text_terms[-step], "blk", -1)
    grad_y = text_terms[0] + carried + returned
    grad_x, sums = (
        lax.psum_scatter(grad_group, "grp", scatter_dimension=0, tiled=True),
        lax.psum_scatter(group_sums, "grp", scatter_dimension=0, tiled=True),
    )
    row_loss = sums / ((2 * REACH + 1) * group)
    return (row_loss, unnormed(grad_x, unit_x, scale_x), unnormed(grad_y, unit_y, scale_y))


def solution(mesh):
    placed = (P(("blk", "grp"), None), P(("blk", "grp"), None), P(), P(), P(("blk", "grp")))
    return jax.shard_map(
        shards,
        mesh=mesh,
        in_specs=placed,
        out_specs=(P(("blk", "grp")), P(("blk", "grp"), None), P(("blk", "grp"), None)),
        check_vma=False,
    )
```

profile of v0, /device:TPU:1, one launch (start us, length us, event | category | flops | bytes accessed | tf_op | source)
XLA Modules:
  0.0 62.6 jit_solution(8459419432554972889)
XLA Ops:
  7.2 0.0 copy-start.1
  7.2 0.0 reduce-scatter.2.cloned.1.call-start
  7.2 1.1 %multiply_reduce_fusion.2 = f32[128]{0:T(128)S(1)} fusion(f32[128,768]{1,0:T(8,128)} %param.6), kind=kLoop, calls=%fused_computation.19 | loop fusion | flops 196480 | bytes 393728 | tf_op jit(solution)/shard_map/reduce_sum | solution.py:15
  8.4 0.0 copy-done.1
  8.4 0.0 copy-start
  8.4 0.1 broadcast_multiply_fusion
  8.5 0.1 collective-permute-start.1
  8.6 2.7 %collective-permute-start = (f32[128,768]{1,0:T(8,128)S(1)}, f32[128,768]{1,0:T(8,128)S(1)}, u32[]{:S(2)}, u32[]{:S(2)}) collective-permute-start(f32[128,768]{1,0:T(8,128)S(1)} %broadcast_multiply_fusion), channel_id=1, source_target_pairs={{0,2},{2,4},{4,6},{6,8},{8,10},{10,12},{12,14},{14,16},{16,18},{18... | collective-permute-start | bytes 1179656 | tf_op jit(solution)/shard_map/ppermute | solution.py:11
  11.9 0.0 copy-done
  11.9 0.1 multiply_reduce_fusion.3
  12.0 0.1 broadcast_multiply_fusion.1
  12.1 8.5 %all_gather.6 = f32[256,768]{1,0:T(8,128)S(1)} all-gather(f32[128,768]{1,0:T(8,128)S(1)} %broadcast_multiply_fusion.1), channel_id=1, replica_groups=mesh['blk'=16,'grp'=2] {'grp'}, dimensions={0}, use_global_device_ids=true | all-gather | bytes 1179648 | tf_op jit(solution)/shard_map/all_gather | solution.py:43
  21.4 0.0 copy-start.3
  21.4 0.6 %copy-done.3 = f32[128]{0:T(128)S(1)} copy-done((f32[128]{0:T(128)S(1)}, f32[128]{0:T(128)}, u32[]{:S(2)}) %copy-start.3) | copy-done | bytes 536
  22.0 3.1 %all-gather = f32[2,1,128]{2,1,0:T(1,128)S(1)} all-gather(f32[1,1,128]{2,1,0:T(1,128)S(1)} %bitcast.26), channel_id=1, replica_groups=mesh['blk'=16,'grp'=2] {'grp'}, dimensions={0}, use_global_device_ids=true | all-gather | bytes 1536 | tf_op jit(solution)/shard_map/all_gather | solution.py:44
  25.1 1.0 %fusion.9 = (f32[256]{0:T(256)S(1)}, f32[256,128]{0,1:T(8,128)S(1)}) fusion(f32[]{:T(128)} %bitcast.19, f32[256,768]{1,0:T(8,128)S(1)} %all_gather.6, f32[128,768]{1,0:T(8,128)S(1)} %broadcast_multiply_fusion, f32[]{:T(128)} %bitcast, s32[128]{0:T(128)S(1)} %iota_add_fusion), kind=kOutput, calls=%fused_computation.27 | convolution fusion | flops 302415616 | bytes 1312264 | tf_op jit(solution)/shard_map/id,jd->ij/dot_general | solution.py:25
  26.1 0.9 %fusion.16 = f32[256,768]{1,0:T(8,128)S(1)} fusion(f32[128,768]{1,0:T(8,128)S(1)} %broadcast_multiply_fusion, f32[256,128]{0,1:T(8,128)S(1)} %get-tuple-element.8, f32[256]{0:T(256)S(1)} %bitcast.20, s32[128]{0:T(128)S(1)} %iota_add_fusion), kind=kOutput, calls=%fused_computation.44 | convolution fusion | flops 302252032 | bytes 1312256 | tf_op jit(solution)/shard_map/dot_general | solution.py:66
  27.0 0.0 collective-permute-done.1
  27.0 1.0 %fusion.10 = (f32[256]{0:T(256)S(1)}, f32[256,128]{0,1:T(8,128)S(1)}) fusion(f32[]{:T(128)} %bitcast.18, f32[256,768]{1,0:T(8,128)S(1)} %all_gather.6, f32[128,768]{1,0:T(8,128)S(1)} %collective-permute-done.1, f32[]{:T(128)} %bitcast), kind=kOutput, calls=%fused_computation.28 | convolution fusion | flops 302284544 | bytes 1311752 | tf_op jit(solution)/shard_map/id,jd->ij/dot_general | solution.py:25
  28.0 0.8 %fusion.11 = f32[256,768]{1,0:T(8,128)S(1)} fusion(f32[128,768]{1,0:T(8,128)S(1)} %collective-permute-done.1, f32[256,128]{0,1:T(8,128)S(1)} %get-tuple-element.4, f32[256]{0:T(256)S(1)} %bitcast.21), kind=kOutput, calls=%fused_computation.34 | convolution fusion | flops 302120960 | bytes 1311744 | tf_op jit(solution)/shard_map/dot_general | solution.py:66
  28.9 0.0 collective-permute-done
  28.9 1.0 %fusion.8 = (f32[256]{0:T(256)S(1)}, f32[256,128]{0,1:T(8,128)S(1)}) fusion(f32[]{:T(128)} %bitcast.17, f32[256,768]{1,0:T(8,128)S(1)} %all_gather.6, f32[128,768]{1,0:T(8,128)S(1)} %collective-permute-done, f32[]{:T(128)} %bitcast), kind=kOutput, calls=%fused_computation.26 | convolution fusion | flops 302284544 | bytes 1311752 | tf_op jit(solution)/shard_map/id,jd->ij/dot_general | solution.py:25
  29.9 1.7 %fusion.1 = f32[256,768]{1,0:T(8,128)} fusion(f32[256,768]{1,0:T(8,128)S(1)} %fusion.11, f32[256,768]{1,0:T(8,128)S(1)} %fusion.16, f32[128,768]{1,0:T(8,128)S(1)} %collective-permute-done, f32[]{:T(128)} %bitcast, f32[256,128]{0,1:T(8,128)S(1)} %get-tuple-element.6, f32[256]{0:T(256)S(1)} %bitcast.22), kind=kOutput, calls=%fused_computation.2 | convolution fusion | flops 302710784 | bytes 2884612 | tf_op jit(solution)/shard_map/dot_general | solution.py:66
  31.6 0.0 reduce-scatter.2.cloned.1.call-update
  31.6 1.3 %convolution_multiply_fusion = f32[128,768]{1,0:T(8,128)} fusion(f32[256,768]{1,0:T(8,128)S(1)} %all_gather.6, f32[]{:T(128)} %bitcast, f32[256,128]{0,1:T(8,128)S(1)} %get-tuple-element.6, f32[256]{0:T(256)S(1)} %bitcast.23), kind=kOutput, calls=%fused_computation.3 | convolution fusion | flops 302219264 | bytes 1311748 | tf_op jit(solution)/shard_map/ij,id->jd/dot_general | solution.py:69
  33.0 0.6 convolution_multiply_fusion.1
  33.5 4.9 %collective-permute-start.3 = (f32[128,768]{1,0:T(8,128)}, f32[128,768]{1,0:T(8,128)S(1)}, u32[]{:S(2)}, u32[]{:S(2)}) collective-permute-start(f32[128,768]{1,0:T(8,128)} %convolution_multiply_fusion), channel_id=1, source_target_pairs={{0,30},{2,0},{4,2},{6,4},{8,6},{10,8},{12,10},{14,12},{16,14},{18,... | collective-permute-start | bytes 1179656 | tf_op jit(solution)/shard_map/ppermute | solution.py:11
  38.4 0.0 collective-permute-start.2
  38.4 0.0 copy-start.4
  38.4 0.7 %copy-done.4 = u32[32]{0:T(128)S(1)} copy-done((u32[32]{0:T(128)S(1)}, u32[32]{0:T(128)}, u32[]{:S(2)}) %copy-start.4) | copy-done | bytes 152
  39.1 0.6 dynamic-slice
  40.3 3.8 %all-reduce = f32[256]{0:T(256)S(1)} all-reduce(f32[256]{0:T(256)S(1)} %add_add_fusion), channel_id=2, replica_groups=mesh['blk'=16,'grp'=2] {'grp'}, use_global_device_ids=true, to_apply=%region_5.6.clone | all-reduce | flops 256 | bytes 2048
  44.1 0.6 dynamic-slice_multiply_fusion
  44.7 0.0 collective-permute-done.3
  44.7 2.7 %collective-permute-done.2 = f32[128,768]{1,0:T(8,128)S(1)} collective-permute-done((f32[128,768]{1,0:T(8,128)S(1)}, f32[128,768]{1,0:T(8,128)S(1)}, u32[]{:S(2)}, u32[]{:S(2)}) %collective-permute-start.2) | collective-permute-done | bytes 393248 | tf_op jit(solution)/shard_map/ppermute | solution.py:11
  47.4 0.7 %multiply_reduce_fusion = (f32[128]{0:T(128)S(1)}, f32[128,768]{1,0:T(8,128)S(1)}) fusion(f32[128,768]{1,0:T(8,128)S(1)} %broadcast_multiply_fusion, f32[128,768]{1,0:T(8,128)S(1)} %collective-permute-done.3, f32[128,768]{1,0:T(8,128)S(1)} %collective-permute-done.2, f32[256,768]{1,0:T(8,128)S(1)} %all_gather.6, f32[256,128]{0,1:T(8,128)S(1)} %get-tuple-element.8, ...), kind=kOutput, calls=%fused_computation.16 | convolution fusion | flops 302743424 | bytes 2492420 | tf_op jit(solution)/shard_map/ij,id->jd/dot_general | solution.py:69
  48.1 0.9 %subtract_multiply_fusion = f32[128,768]{1,0:T(8,128)} fusion(f32[128,768]{1,0:T(8,128)S(1)} %get-tuple-element.10, f32[128]{0:T(128)S(1)} %get-tuple-element.9, f32[128]{0:T(128)S(1)} %add_rsqrt_fusion, f32[128,768]{1,0:T(8,128)S(1)} %copy-done.1), kind=kLoop, calls=%fused_computation.15 | loop fusion | flops 393216 | bytes 1180672 | tf_op jit(solution)/shard_map/mul | solution.py:20
  49.0 4.7 %reduce-scatter.2.cloned.1.call-done = f32[128,768]{1,0:T(8,128)} async-done(((f32[256,768]{1,0:T(8,128)}), f32[128,768]{1,0:T(8,128)}) %reduce-scatter.2.cloned.1.call-update) | async-done | bytes 393232 | tf_op jit(solution)/shard_map/reduce_scatter | solution.py:78
  53.6 0.0 copy-start.2
  53.6 1.2 %multiply_reduce_fusion.1 = f32[128]{0:T(128)S(1)} fusion(f32[128,768]{1,0:T(8,128)} %reduce-scatter.2.cloned.1.call-done, f32[128,768]{1,0:T(8,128)S(1)} %copy-done, f32[128]{0:T(128)S(1)} %add_rsqrt_fusion.1), kind=kLoop, calls=%fused_computation.18 | loop fusion | flops 294784 | bytes 787456 | tf_op jit(solution)/shard_map/reduce_sum | solution.py:20
  54.9 0.0 copy-done.2
  54.9 0.9 %subtract_multiply_fusion.1 = f32[128,768]{1,0:T(8,128)} fusion(f32[128,768]{1,0:T(8,128)S(1)} %copy-done.2, f32[128]{0:T(128)S(1)} %multiply_reduce_fusion.1, f32[128]{0:T(128)S(1)} %add_rsqrt_fusion.1, f32[128,768]{1,0:T(8,128)S(1)} %copy-done), kind=kLoop, calls=%fused_computation.17 | loop fusion | flops 393216 | bytes 1180672 | tf_op jit(solution)/shard_map/mul | solution.py:20
  (4 shorter events, 0.0 us)
Async XLA Ops:
  7.2 1.2 %copy-start.1 = (f32[128,768]{1,0:T(8,128)S(1)}, f32[128,768]{1,0:T(8,128)}, u32[]{:S(2)}) copy-start(f32[128,768]{1,0:T(8,128)} %param.6) | copy-start | bytes 1179652
  7.2 46.5 %reduce-scatter.2.cloned.1.call-start = ((), (), s32[]{:S(2)}) async-start(), calls=%async_computation.1 | async-start | bytes 1179648 | tf_op jit(solution)/shard_map/reduce_scatter | solution.py:78
  8.4 3.5 %copy-start = (f32[128,768]{1,0:T(8,128)S(1)}, f32[128,768]{1,0:T(8,128)}, u32[]{:S(2)}) copy-start(f32[128,768]{1,0:T(8,128)} %param.5) | copy-start | bytes 1179652
  8.5 18.5 %collective-permute-start.1 = (f32[128,768]{1,0:T(8,128)S(1)}, f32[128,768]{1,0:T(8,128)S(1)}, u32[]{:S(2)}, u32[]{:S(2)}) collective-permute-start(f32[128,768]{1,0:T(8,128)S(1)} %broadcast_multiply_fusion), channel_id=1, source_target_pairs={{0,30},{2,0},{4,2},{6,4},{8,6},{10,8},{12,10},{14,12},{16,14},{18,... | collective-permute-start | bytes 1179656 | tf_op jit(solution)/shard_map/ppermute | solution.py:11
  8.6 20.3 %collective-permute-start = (f32[128,768]{1,0:T(8,128)S(1)}, f32[128,768]{1,0:T(8,128)S(1)}, u32[]{:S(2)}, u32[]{:S(2)}) collective-permute-start(f32[128,768]{1,0:T(8,128)S(1)} %broadcast_multiply_fusion), channel_id=1, source_target_pairs={{0,2},{2,4},{4,6},{6,8},{8,10},{10,12},{12,14},{14,16},{16,18},{18... | collective-permute-start | bytes 1179656 | tf_op jit(solution)/shard_map/ppermute | solution.py:11
  21.4 0.7 %copy-start.3 = (f32[128]{0:T(128)S(1)}, f32[128]{0:T(128)}, u32[]{:S(2)}) copy-start(f32[128]{0:T(128)} %param.9) | copy-start | bytes 1540
  33.5 11.2 %collective-permute-start.3 = (f32[128,768]{1,0:T(8,128)}, f32[128,768]{1,0:T(8,128)S(1)}, u32[]{:S(2)}, u32[]{:S(2)}) collective-permute-start(f32[128,768]{1,0:T(8,128)} %convolution_multiply_fusion), channel_id=1, source_target_pairs={{0,30},{2,0},{4,2},{6,4},{8,6},{10,8},{12,10},{14,12},{16,14},{18,... | collective-permute-start | bytes 1179656 | tf_op jit(solution)/shard_map/ppermute | solution.py:11
  38.4 8.9 %collective-permute-start.2 = (f32[128,768]{1,0:T(8,128)S(1)}, f32[128,768]{1,0:T(8,128)S(1)}, u32[]{:S(2)}, u32[]{:S(2)}) collective-permute-start(f32[128,768]{1,0:T(8,128)S(1)} %convolution_multiply_fusion.1), channel_id=1, source_target_pairs={{0,2},{2,4},{4,6},{6,8},{8,10},{10,12},{12,14},{14,16},{16,18},{18... | collective-permute-start | bytes 1179656 | tf_op jit(solution)/shard_map/ppermute | solution.py:11
  38.4 0.7 %copy-start.4 = (u32[32]{0:T(128)S(1)}, u32[32]{0:T(128)}, u32[]{:S(2)}) copy-start(u32[32]{0:T(128)} %constant.26) | copy-start | bytes 388
  53.6 1.3 %copy-start.2 = (f32[128,768]{1,0:T(8,128)S(1)}, f32[128,768]{1,0:T(8,128)}, u32[]{:S(2)}) copy-start(f32[128,768]{1,0:T(8,128)} %reduce-scatter.2.cloned.1.call-done) | copy-start | bytes 1179652
Sparse Core Ops, SparseCore 0:
  31.7 21.8 reduce-scatter.1
where the time goes:
time: 63.7 us; the launch traced here: 62.6 us
  between operations  16.2 us (25%)
  blocking collectives  15.4 us (24%)
  matrix products  9.09 us (14%)
  starting transfers between devices  7.65 us (12%)
  waiting for transfers between devices  7.36 us (12%)
  other arithmetic  5.08 us (8%)
  local copies, waits for them, and re-layouts  1.9 us (3%)
    all_gather x1, blocking collectives, shards(): lax.all_gather(unit_x, 'grp', axis=0, tiled=True)  8.52 us
    ppermute x4, starting transfers between devices, passed_along(): lax.ppermute(x, axis, [(i, (i + by) % length) for i in range(length)])  7.62 us
    reduce_scatter x1, waiting for transfers between devices, shards(): lax.psum_scatter(grad_group, 'grp', scatter_dimension=0, tiled=True)  4.67 us
    unnamed x1, blocking collectives  3.78 us
    dot_general x3, matrix products, shards(): jnp.dot(slope, window[offset], precision=lax.Precision.HIGHEST)  3.45 us
    all_gather x1, blocking collectives, shards(): lax.all_gather(row_weight, 'grp', axis=0, tiled=True)  3.07 us
    dot_general x3, matrix products, tile_terms(): jnp.einsum('id,jd->ij', left, right, precision=lax.Precision.HIGHEST)  2.99 us
    ppermute x4, waiting for transfers between devices, passed_along(): lax.ppermute(x, axis, [(i, (i + by) % length) for i in range(length)])  2.67 us
  transfers between devices with their start and end apart: 5, of which 2 were waited for; matrix products, arithmetic and copies ran while one was open for 14% of the time, Pallas kernels for 0%

commit v1 on v0

v1 whole, which is shorter than its diff:
```python
import jax
import jax.numpy as jnp
from jax import lax
from jax.sharding import PartitionSpec as P

HIGH = lax.Precision.HIGH


def swapped(x, axis, near):
    length = lax.axis_size(axis)
    if near:
        pairs = [(i, i + 1) for i in range(0, length, 2)]
    else:
        pairs = [(i, (i + 1) % length) for i in range(1, length, 2)]
    return lax.ppermute(x, axis, pairs + [(b, a) for (a, b) in pairs])


def shifted(x, axis, by):
    length = lax.axis_size(axis)
    return lax.ppermute(x, axis, [(i, (i + by) % length) for i in range(length)])


def normed(values):
    scale = lax.rsqrt(jnp.sum(values * values, axis=1, keepdims=True) + 1e-06)
    return (values * scale, scale)


def unnormed(grad, unit, scale):
    return scale * (grad - unit * jnp.sum(unit * grad, axis=1, keepdims=True))


def tile_terms(left, right, temper, offset_b, weight, positive):
    logits = temper * jnp.einsum("id,jd->ij", left, right, precision=HIGH) + offset_b
    signed = logits if positive is None else jnp.where(positive, -logits, logits)
    losses = jax.nn.softplus(signed)
    slope = jax.nn.sigmoid(signed) * weight[:, None]
    if positive is not None:
        slope = jnp.where(positive, -slope, slope)
    return (jnp.sum(losses, axis=1), slope)


def shards(images, texts, log_temp, bias, row_weight):
    members = lax.axis_size("grp")
    count = images.shape[0]
    rows_i = [images] + [shifted(images, "grp", -s) for s in range(1, members)]
    weights = [row_weight] + [shifted(row_weight, "grp", -s) for s in range(1, members)]
    far = swapped(texts, "blk", False)
    near = swapped(texts, "blk", True)
    temper = jnp.exp(log_temp[0])
    offset_b = bias[0]
    unit_y, scale_y = normed(texts)
    unit_near, _ = normed(near)
    unit_far, _ = normed(far)
    units_x, scales_x = zip(*[normed(r) for r in rows_i])
    eye = lax.broadcasted_iota(jnp.int32, (count, count), 0) == lax.broadcasted_iota(
        jnp.int32, (count, count), 1
    )
    texts_all = [unit_y, unit_near, unit_far]
    grad_t = [None, None, None]
    grads_x = []
    sums_x = []
    for s in range(members):
        total = None
        grad = None
        for t in range(3):
            positive = eye if (s == 0 and t == 0) else None
            part, slope = tile_terms(
                units_x[s], texts_all[t], temper, offset_b, weights[s], positive
            )
            slope = slope * temper
            total = part if total is None else total + part
            g = jnp.dot(slope, texts_all[t], precision=HIGH)
            grad = g if grad is None else grad + g
            h = jnp.einsum("ij,id->jd", slope, units_x[s], precision=HIGH)
            grad_t[t] = h if grad_t[t] is None else grad_t[t] + h
        grads_x.append(grad)
        sums_x.append(total)
    back_far = swapped(grad_t[2], "blk", False)
    back_near = swapped(grad_t[1], "blk", True)
    grad_x = grads_x[0]
    sums = sums_x[0]
    for s in range(1, members):
        grad_x = grad_x + shifted(grads_x[s], "grp", s)
        sums = sums + shifted(sums_x[s], "grp", s)
    grad_y = grad_t[0] + back_near + back_far
    row_loss = sums / (3 * members * count)
    return (row_loss, unnormed(grad_x, units_x[0], scales_x[0]), unnormed(grad_y, unit_y, scale_y))


def solution(mesh):
    placed = (P(("blk", "grp"), None), P(("blk", "grp"), None), P(), P(), P(("blk", "grp")))
    return jax.shard_map(
        shards,
        mesh=mesh,
        in_specs=placed,
        out_specs=(P(("blk", "grp")), P(("blk", "grp"), None), P(("blk", "grp"), None)),
        check_vma=False,
    )
```

time: 63.7 us -> 35.9 us (0.56); the launches traced: 62.6 us -> 35.7 us
  blocking collectives: 15.4 us -> 0 us
  between operations: 16.2 us -> 2.19 us
  waiting for transfers between devices: 7.36 us -> 11.1 us
  starting transfers between devices: 7.65 us -> 10.2 us
  matrix products: 9.09 us -> 7.74 us
  local copies, waits for them, and re-layouts: 1.9 us -> 0.66 us
  other arithmetic: 5.08 us -> 3.88 us
    all_gather x2 -> x0, blocking collectives: 11.6 us -> none  [the longest x1 8.52 us: shards(): lax.all_gather(unit_x, 'grp', axis=0, tiled=True)]
    ppermute x4 -> x8, waiting for transfers between devices: 2.67 us -> 11.1 us  [the longest x4 7.74 us: shifted(): lax.ppermute(x, axis, [(i, (i + by) % length) for i in range(length)])]
    reduce_scatter x1 -> x0, waiting for transfers between devices: 4.67 us -> none  [shards(): lax.psum_scatter(grad_group, 'grp', scatter_dimension=0, tiled=True)]
    unnamed x1 -> x0, blocking collectives: 3.78 us -> none
    ppermute x4 -> x8, starting transfers between devices: 7.62 us -> 10.2 us  [the longest x4 7.11 us: swapped(): return lax.ppermute(x, axis, pairs + [(b, a) for a, b in pairs])]
    dot_general x9 -> x18, matrix products: 9.09 us -> 7.74 us  [the longest x6 2.8 us: tile_terms(): jnp.einsum('id,jd->ij', left, right, precision=HIGH)]
    reduce_sum x1 -> x0, other arithmetic: 1.25 us -> none  [unnormed(): return scale * (grad - unit * jnp.sum(unit * grad, axis=1, keepdims=True))]
    unnamed x11 -> x6, local copies, waits for them, and re-layouts: 1.9 us -> 0.66 us
  transfers between devices with their start and end apart: 5 -> 8, of which waited for: 2 -> 4; matrix products, arithmetic and copies ran while one was open for 14% -> 29% of each run, Pallas kernels for 0% -> 0%
where the time goes in v1:
time: 35.9 us; the launch traced here: 35.7 us
  waiting for transfers between devices  11.1 us (31%)
  starting transfers between devices  10.2 us (28%)
  matrix products  7.74 us (22%)
  other arithmetic  3.88 us (11%)
  between operations  2.19 us (6%)
  local copies, waits for them, and re-layouts  0.66 us (2%)
    ppermute x4, waiting for transfers between devices, shifted(): lax.ppermute(x, axis, [(i, (i + by) % length) for i in range(length)])  7.74 us
    ppermute x4, starting transfers between devices, swapped(): return lax.ppermute(x, axis, pairs + [(b, a) for a, b in pairs])  7.11 us
    ppermute x4, waiting for transfers between devices, swapped(): return lax.ppermute(x, axis, pairs + [(b, a) for a, b in pairs])  3.35 us
    ppermute x4, starting transfers between devices, shifted(): lax.ppermute(x, axis, [(i, (i + by) % length) for i in range(length)])  3.06 us
    dot_general x6, matrix products, tile_terms(): jnp.einsum('id,jd->ij', left, right, precision=HIGH)  2.8 us
    dot_general x6, matrix products, shards(): g = jnp.dot(slope, texts_all[t], precision=HIGH)  2.5 us
    dot_general x6, matrix products, shards(): h = jnp.einsum('ij,id->jd', slope, units_x[s], precision=HIGH)  2.45 us
    mul x2, other arithmetic, unnormed(): return scale * (grad - unit * jnp.sum(unit * grad, axis=1, keepdims=True))  1.79 us
  transfers between devices with their start and end apart: 8, of which 4 were waited for; matrix products, arithmetic and copies ran while one was open for 29% of the time, Pallas kernels for 0%

profile of v1, /device:TPU:1, one launch (start us, length us, event | category | flops | bytes accessed | tf_op | source)
XLA Modules:
  0.0 35.7 jit_solution(6203607005374340771)
XLA Ops:
  0.6 0.0 copy-start
  0.6 0.0 copy-start.1
  0.6 2.7 %collective-permute-start.1 = (f32[128,768]{1,0:T(8,128)}, f32[128,768]{1,0:T(8,128)S(1)}, u32[]{:S(2)}, u32[]{:S(2)}) collective-permute-start(f32[128,768]{1,0:T(8,128)} %param.6), channel_id=1, source_target_pairs={{2,4},{6,8},{10,12},{14,16},{18,20},{22,24},{26,28},{30,0},{4,2},{... | collective-permute-start | bytes 1179656 | tf_op jit(solution)/shard_map/ppermute | solution.py:15
  3.3 2.9 %collective-permute-start = (f32[128,768]{1,0:T(8,128)}, f32[128,768]{1,0:T(8,128)S(1)}, u32[]{:S(2)}, u32[]{:S(2)}) collective-permute-start(f32[128,768]{1,0:T(8,128)} %param.6), channel_id=1, source_target_pairs={{0,2},{4,6},{8,10},{12,14},{16,18},{20,22},{24,26},{28,30},{2,0},{... | collective-permute-start | bytes 1179656 | tf_op jit(solution)/shard_map/ppermute | solution.py:15
  6.2 1.2 %collective-permute-start.2 = (f32[128,768]{1,0:T(8,128)}, f32[128,768]{1,0:T(8,128)S(1)}, u32[]{:S(2)}, u32[]{:S(2)}) collective-permute-start(f32[128,768]{1,0:T(8,128)} %param.5), channel_id=1, source_target_pairs={{0,1},{1,0},{2,3},{3,2},{4,5},{5,4},{6,7},{7,6},{8,9},{9,8},{10,11... | collective-permute-start | bytes 1179656 | tf_op jit(solution)/shard_map/ppermute | solution.py:20
  7.4 0.3 collective-permute-start.4
  7.7 1.1 %multiply_reduce_fusion.5 = f32[128]{0:T(128)S(1)} fusion(f32[128,768]{1,0:T(8,128)} %param.6), kind=kLoop, calls=%fused_computation.29 | loop fusion | flops 196480 | bytes 393728 | tf_op jit(solution)/shard_map/reduce_sum | solution.py:24
  8.8 0.0 copy-done
  8.8 0.1 multiply_reduce_fusion.6
  10.3 0.0 copy-done.1
  10.3 0.5 %fusion.69 = (f32[128]{0:T(128)S(1)}, f32[128,128]{0,1:T(8,128)S(1)}) fusion(f32[]{:T(128)} %bitcast.2, f32[128,768]{1,0:T(8,128)S(1)} %copy-done.1, f32[128]{0:T(128)S(1)} %add_rsqrt_fusion.3, f32[128,768]{1,0:T(8,128)S(1)} %copy-done, f32[128]{0:T(128)S(1)} %add_rsqrt_fusion.4, f32[]{:T(128)} %bitcast), kind=kOutput, calls=%fused_computation.94 | convolution fusion | flops 75890560 | bytes 853512 | tf_op jit(solution)/shard_map/id,jd->ij/dot_general | solution.py:33
  10.8 0.0 copy-start.2
  10.8 0.7 %copy-done.2 = f32[128]{0:T(128)S(1)} copy-done((f32[128]{0:T(128)S(1)}, f32[128]{0:T(128)}, u32[]{:S(2)}) %copy-start.2) | copy-done | bytes 536
  11.4 0.4 %fusion.27 = f32[128,768]{1,0:T(8,128)S(1)} fusion(f32[128,768]{1,0:T(8,128)S(1)} %copy-done.1, f32[128]{0:T(128)S(1)} %add_rsqrt_fusion.3, f32[128,128]{0,1:T(8,128)S(1)} %get-tuple-element.12, f32[128]{0:T(128)S(1)} %copy-done.2, f32[]{:T(128)} %bitcast), kind=kOutput, calls=%fused_computation.48 | convolution fusion | flops 75726848 | bytes 852996 | tf_op jit(solution)/shard_map/dot_general | solution.py:72
  11.8 0.4 %fusion.35 = f32[128,768]{1,0:T(8,128)S(1)} fusion(f32[128,768]{1,0:T(8,128)S(1)} %copy-done, f32[128]{0:T(128)S(1)} %add_rsqrt_fusion.4, f32[128,128]{0,1:T(8,128)S(1)} %get-tuple-element.12, f32[128]{0:T(128)S(1)} %copy-done.2, f32[]{:T(128)} %bitcast), kind=kOutput, calls=%fused_computation.56 | convolution fusion | flops 75726848 | bytes 852996 | tf_op jit(solution)/shard_map/ij,id->jd/dot_general | solution.py:74
  12.2 1.3 %collective-permute-done.1 = f32[128,768]{1,0:T(8,128)S(1)} collective-permute-done((f32[128,768]{1,0:T(8,128)}, f32[128,768]{1,0:T(8,128)S(1)}, u32[]{:S(2)}, u32[]{:S(2)}) %collective-permute-start.1) | collective-permute-done | bytes 393248 | tf_op jit(solution)/shard_map/ppermute | solution.py:15
  13.5 0.1 multiply_reduce_fusion.3
  13.6 3.4 %collective-permute-done.2 = f32[128,768]{1,0:T(8,128)S(1)} collective-permute-done((f32[128,768]{1,0:T(8,128)}, f32[128,768]{1,0:T(8,128)S(1)}, u32[]{:S(2)}, u32[]{:S(2)}) %collective-permute-start.2) | collective-permute-done | bytes 393248 | tf_op jit(solution)/shard_map/ppermute | solution.py:20
  17.1 0.1 multiply_reduce_fusion.2
  17.2 0.0 collective-permute-done
  17.2 0.1 multiply_reduce_fusion.4
  17.3 0.5 %fusion.72 = (f32[128]{0:T(128)S(1)}, f32[128,128]{0,1:T(8,128)S(1)}) fusion(f32[]{:T(128)} %bitcast.5, f32[128,768]{1,0:T(8,128)S(1)} %copy-done.1, f32[128]{0:T(128)S(1)} %add_rsqrt_fusion.3, f32[128,768]{1,0:T(8,128)S(1)} %collective-permute-done.2, f32[128]{0:T(128)S(1)} %add_rsqrt_fusion, f32[]{:T(128)} %bitcast), kind=kOutput, calls=%fused_computation.97 | convolution fusion | flops 75841408 | bytes 853512 | tf_op jit(solution)/shard_map/id,jd->ij/dot_general | solution.py:33
  17.8 0.5 %fusion.74 = (f32[128]{0:T(128)S(1)}, f32[128,128]{0,1:T(8,128)S(1)}) fusion(f32[]{:T(128)} %bitcast.3, f32[128,768]{1,0:T(8,128)S(1)} %collective-permute-done.1, f32[128]{0:T(128)S(1)} %add_rsqrt_fusion.1, f32[128,768]{1,0:T(8,128)S(1)} %collective-permute-done.2, f32[128]{0:T(128)S(1)} %add_rsqrt_fusion, f32[]{:T(128)} %bitcast), kind=kOutput, calls=%fused_computation.99 | convolution fusion | flops 75841408 | bytes 853512 | tf_op jit(solution)/shard_map/id,jd->ij/dot_general | solution.py:33
  18.3 0.5 %fusion.73 = (f32[128]{0:T(128)S(1)}, f32[128,128]{0,1:T(8,128)S(1)}) fusion(f32[]{:T(128)} %bitcast.4, f32[128,768]{1,0:T(8,128)S(1)} %collective-permute-done, f32[128]{0:T(128)S(1)} %add_rsqrt_fusion.2, f32[128,768]{1,0:T(8,128)S(1)} %collective-permute-done.2, f32[128]{0:T(128)S(1)} %add_rsqrt_fusion, f32[]{:T(128)} %bitcast), kind=kOutput, calls=%fused_computation.98 | convolution fusion | flops 75841408 | bytes 853512 | tf_op jit(solution)/shard_map/id,jd->ij/dot_general | solution.py:33
  18.8 1.3 %collective-permute-start.3 = (f32[128]{0:T(128)S(1)}, f32[128]{0:T(128)S(1)}, u32[]{:S(2)}, u32[]{:S(2)}) collective-permute-start(f32[128]{0:T(128)S(1)} %add_add_fusion), channel_id=1, source_target_pairs={{0,1},{1,0},{2,3},{3,2},{4,5},{5,4},{6,7},{7,6},{8,9},{9,8},{10,11... | collective-permute-start | bytes 1544 | tf_op jit(solution)/shard_map/ppermute | solution.py:20
  20.0 0.0 collective-permute-done.4
  20.0 0.4 %fusion.10 = f32[128,768]{1,0:T(8,128)S(1)} fusion(f32[128,768]{1,0:T(8,128)S(1)} %collective-permute-done.1, f32[128]{0:T(128)S(1)} %add_rsqrt_fusion.1, f32[128,128]{0,1:T(8,128)S(1)} %get-tuple-element.4, f32[128]{0:T(128)S(1)} %collective-permute-done.4, f32[]{:T(128)} %bitcast), kind=kOutput, calls=%fused_computation.31 | convolution fusion | flops 75677696 | bytes 852996 | tf_op jit(solution)/shard_map/dot_general | solution.py:72
  20.4 0.4 %fusion.15 = f32[128,768]{1,0:T(8,128)S(1)} fusion(f32[128,768]{1,0:T(8,128)S(1)} %collective-permute-done, f32[128]{0:T(128)S(1)} %add_rsqrt_fusion.2, f32[128,128]{0,1:T(8,128)S(1)} %get-tuple-element.8, f32[128]{0:T(128)S(1)} %collective-permute-done.4, f32[]{:T(128)} %bitcast), kind=kOutput, calls=%fused_computation.36 | convolution fusion | flops 75677696 | bytes 852996 | tf_op jit(solution)/shard_map/dot_general | solution.py:72
  20.8 0.4 %fusion.1 = f32[128,768]{1,0:T(8,128)S(1)} fusion(f32[128,768]{1,0:T(8,128)S(1)} %fusion.10, f32[128,768]{1,0:T(8,128)S(1)} %fusion.15, f32[128,768]{1,0:T(8,128)S(1)} %copy-done.1, f32[128]{0:T(128)S(1)} %add_rsqrt_fusion.3, f32[128,128]{0,1:T(8,128)S(1)} %get-tuple-element.6, f32[128]{0:T(128)S(1)} %collective-permute-done.4, f32[]{:T(128)} %bitcast), kind=kOutput, calls=%fused_computation.7 | convolution fusion | flops 75874304 | bytes 1639428 | tf_op jit(solution)/shard_map/dot_general | solution.py:72
  21.3 0.3 collective-permute-start.5
  21.6 0.5 %fusion.71 = (f32[128]{0:T(128)S(1)}, f32[128,128]{0,1:T(8,128)S(1)}) fusion(f32[]{:T(128)} %bitcast.6, f32[128,768]{1,0:T(8,128)S(1)} %collective-permute-done.1, f32[128]{0:T(128)S(1)} %add_rsqrt_fusion.1, f32[128,768]{1,0:T(8,128)S(1)} %copy-done, f32[128]{0:T(128)S(1)} %add_rsqrt_fusion.4, f32[]{:T(128)} %bitcast), kind=kOutput, calls=%fused_computation.96 | convolution fusion | flops 75841408 | bytes 853512 | tf_op jit(solution)/shard_map/id,jd->ij/dot_general | solution.py:33
  22.0 0.4 %fusion.31 = f32[128,768]{1,0:T(8,128)S(1)} fusion(f32[128,768]{1,0:T(8,128)S(1)} %copy-done, f32[128]{0:T(128)S(1)} %add_rsqrt_fusion.4, f32[128,128]{0,1:T(8,128)S(1)} %get-tuple-element.10, f32[128]{0:T(128)S(1)} %copy-done.2, f32[]{:T(128)} %bitcast), kind=kOutput, calls=%fused_computation.52 | convolution fusion | flops 75677696 | bytes 852996 | tf_op jit(solution)/shard_map/ij,id->jd/dot_general | solution.py:74
  22.4 0.4 %convolution_add_fusion = f32[128,768]{1,0:T(8,128)S(1)} fusion(f32[128,768]{1,0:T(8,128)S(1)} %fusion.31, f32[128,768]{1,0:T(8,128)S(1)} %collective-permute-done.2, f32[128]{0:T(128)S(1)} %add_rsqrt_fusion, f32[128,128]{0,1:T(8,128)S(1)} %get-tuple-element.4, f32[128]{0:T(128)S(1)} %collective-permute-done.4, f32[]{:T(128)} %bitcast), kind=kOutput, calls=%fused_computation | convolution fusion | flops 75776000 | bytes 1246212 | tf_op jit(solution)/shard_map/ij,id->jd/dot_general | solution.py:74
  22.8 0.1 collective-permute-start.7
  22.9 0.5 %fusion.70 = (f32[128]{0:T(128)S(1)}, f32[128,128]{0,1:T(8,128)S(1)}) fusion(f32[]{:T(128)} %bitcast.7, f32[128,768]{1,0:T(8,128)S(1)} %collective-permute-done, f32[128]{0:T(128)S(1)} %add_rsqrt_fusion.2, f32[128,768]{1,0:T(8,128)S(1)} %copy-done, f32[128]{0:T(128)S(1)} %add_rsqrt_fusion.4, f32[]{:T(128)} %bitcast), kind=kOutput, calls=%fused_computation.95 | convolution fusion | flops 75841408 | bytes 853512 | tf_op jit(solution)/shard_map/id,jd->ij/dot_general | solution.py:33
  23.4 0.4 %fusion.33 = f32[128,768]{1,0:T(8,128)S(1)} fusion(f32[128,768]{1,0:T(8,128)S(1)} %copy-done, f32[128]{0:T(128)S(1)} %add_rsqrt_fusion.4, f32[128,128]{0,1:T(8,128)S(1)} %get-tuple-element.14, f32[128]{0:T(128)S(1)} %copy-done.2, f32[]{:T(128)} %bitcast), kind=kOutput, calls=%fused_computation.54 | convolution fusion | flops 75677696 | bytes 852996 | tf_op jit(solution)/shard_map/ij,id->jd/dot_general | solution.py:74
  23.8 0.4 %convolution_add_fusion.1 = f32[128,768]{1,0:T(8,128)S(1)} fusion(f32[128,768]{1,0:T(8,128)S(1)} %fusion.33, f32[128,768]{1,0:T(8,128)S(1)} %collective-permute-done.2, f32[128]{0:T(128)S(1)} %add_rsqrt_fusion, f32[128,128]{0,1:T(8,128)S(1)} %get-tuple-element.8, f32[128]{0:T(128)S(1)} %collective-permute-done.4, f32[]{:T(128)} %bitcast), kind=kOutput, calls=%fused_computation.1 | convolution fusion | flops 75776000 | bytes 1246212 | tf_op jit(solution)/shard_map/ij,id->jd/dot_general | solution.py:74
  24.1 1.5 %collective-permute-start.6 = (f32[128,768]{1,0:T(8,128)S(1)}, f32[128,768]{1,0:T(8,128)S(1)}, u32[]{:S(2)}, u32[]{:S(2)}) collective-permute-start(f32[128,768]{1,0:T(8,128)S(1)} %convolution_add_fusion.1), channel_id=1, source_target_pairs={{0,2},{4,6},{8,10},{12,14},{16,18},{20,22},{24,26},{28,30},{2,0},{... | collective-permute-start | bytes 1179656 | tf_op jit(solution)/shard_map/ppermute | solution.py:15
  25.6 0.4 %convolution_add_fusion.5 = f32[128,768]{1,0:T(8,128)S(1)} fusion(f32[128,768]{1,0:T(8,128)S(1)} %fusion.27, f32[128,768]{1,0:T(8,128)S(1)} %collective-permute-done, f32[128]{0:T(128)S(1)} %add_rsqrt_fusion.2, f32[128,128]{0,1:T(8,128)S(1)} %get-tuple-element.14, f32[128]{0:T(128)S(1)} %copy-done.2, f32[]{:T(128)} %bitcast), kind=kOutput, calls=%fused_computation.5 | convolution fusion | flops 75776000 | bytes 1246212 | tf_op jit(solution)/shard_map/dot_general | solution.py:72
  26.0 0.0 collective-permute-done.3
  26.0 0.5 %add_multiply_fusion = f32[128]{0:T(128)} fusion(f32[128]{0:T(128)S(1)} %collective-permute-done.3, f32[128]{0:T(128)S(1)} %get-tuple-element.9, f32[128]{0:T(128)S(1)} %get-tuple-element.11, f32[128]{0:T(128)S(1)} %get-tuple-element.13), kind=kLoop, calls=%fused_computation.106 | loop fusion | flops 512 | bytes 2560 | tf_op jit(solution)/shard_map/div | solution.py:86
  26.6 4.3 %collective-permute-done.5 = f32[128,768]{1,0:T(8,128)S(1)} collective-permute-done((f32[128,768]{1,0:T(8,128)S(1)}, f32[128,768]{1,0:T(8,128)S(1)}, u32[]{:S(2)}, u32[]{:S(2)}) %collective-permute-start.5) | collective-permute-done | bytes 393248 | tf_op jit(solution)/shard_map/ppermute | solution.py:20
  30.8 0.5 %multiply_reduce_fusion.1 = (f32[128]{0:T(128)S(1)}, f32[128,768]{1,0:T(8,128)S(1)}) fusion(f32[128,768]{1,0:T(8,128)S(1)} %copy-done, f32[128]{0:T(128)S(1)} %add_rsqrt_fusion.4, f32[128,768]{1,0:T(8,128)S(1)} %collective-permute-done.5, f32[128,768]{1,0:T(8,128)S(1)} %convolution_add_fusion.5, f32[128,768]{1,0:T(8,128)S(1)} %collective-permute-done.1, ...), kind=kOutput, calls=%fused_computation.25 | convolution fusion | flops 76169088 | bytes 2033668 | tf_op jit(solution)/shard_map/dot_general | solution.py:72
  31.4 0.9 %subtract_multiply_fusion.1 = f32[128,768]{1,0:T(8,128)} fusion(f32[128,768]{1,0:T(8,128)S(1)} %get-tuple-element.16, f32[128,768]{1,0:T(8,128)S(1)} %copy-done, f32[128]{0:T(128)S(1)} %get-tuple-element.15, f32[128]{0:T(128)S(1)} %add_rsqrt_fusion.4), kind=kLoop, calls=%fused_computation.24 | loop fusion | flops 393216 | bytes 1180672 | tf_op jit(solution)/shard_map/mul | solution.py:29
  32.3 2.0 %collective-permute-done.7 = f32[128,768]{1,0:T(8,128)S(1)} collective-permute-done((f32[128,768]{1,0:T(8,128)S(1)}, f32[128,768]{1,0:T(8,128)S(1)}, u32[]{:S(2)}, u32[]{:S(2)}) %collective-permute-start.7) | collective-permute-done | bytes 393248 | tf_op jit(solution)/shard_map/ppermute | solution.py:15
  34.3 0.0 collective-permute-done.6
  34.3 0.5 %multiply_reduce_fusion = (f32[128]{0:T(128)S(1)}, f32[128,768]{1,0:T(8,128)S(1)}) fusion(f32[128,768]{1,0:T(8,128)S(1)} %copy-done.1, f32[128]{0:T(128)S(1)} %add_rsqrt_fusion.3, f32[128,768]{1,0:T(8,128)S(1)} %collective-permute-done.7, f32[128,768]{1,0:T(8,128)S(1)} %collective-permute-done.6, f32[128,768]{1,0:T(8,128)S(1)} %fusion.35, ...), kind=kOutput, calls=%fused_computation.23 | convolution fusion | flops 76267392 | bytes 2426884 | tf_op jit(solution)/shard_map/ij,id->jd/dot_general | solution.py:74
  34.8 0.9 %subtract_multiply_fusion = f32[128,768]{1,0:T(8,128)} fusion(f32[128,768]{1,0:T(8,128)S(1)} %get-tuple-element.18, f32[128,768]{1,0:T(8,128)S(1)} %copy-done.1, f32[128]{0:T(128)S(1)} %get-tuple-element.17, f32[128]{0:T(128)S(1)} %add_rsqrt_fusion.3), kind=kLoop, calls=%fused_computation.22 | loop fusion | flops 393216 | bytes 1180672 | tf_op jit(solution)/shard_map/mul | solution.py:29
  (6 shorter events, 0.0 us)
Async XLA Ops:
  0.6 8.2 %copy-start = (f32[128,768]{1,0:T(8,128)S(1)}, f32[128,768]{1,0:T(8,128)}, u32[]{:S(2)}) copy-start(f32[128,768]{1,0:T(8,128)} %param.5) | copy-start | bytes 1179652
  0.6 9.6 %copy-start.1 = (f32[128,768]{1,0:T(8,128)S(1)}, f32[128,768]{1,0:T(8,128)}, u32[]{:S(2)}) copy-start(f32[128,768]{1,0:T(8,128)} %param.6) | copy-start | bytes 1179652
  0.6 12.9 %collective-permute-start.1 = (f32[128,768]{1,0:T(8,128)}, f32[128,768]{1,0:T(8,128)S(1)}, u32[]{:S(2)}, u32[]{:S(2)}) collective-permute-start(f32[128,768]{1,0:T(8,128)} %param.6), channel_id=1, source_target_pairs={{2,4},{6,8},{10,12},{14,16},{18,20},{22,24},{26,28},{30,0},{4,2},{... | collective-permute-start | bytes 1179656 | tf_op jit(solution)/shard_map/ppermute | solution.py:15
  3.3 13.9 %collective-permute-start = (f32[128,768]{1,0:T(8,128)}, f32[128,768]{1,0:T(8,128)S(1)}, u32[]{:S(2)}, u32[]{:S(2)}) collective-permute-start(f32[128,768]{1,0:T(8,128)} %param.6), channel_id=1, source_target_pairs={{0,2},{4,6},{8,10},{12,14},{16,18},{20,22},{24,26},{28,30},{2,0},{... | collective-permute-start | bytes 1179656 | tf_op jit(solution)/shard_map/ppermute | solution.py:15
  6.2 10.9 %collective-permute-start.2 = (f32[128,768]{1,0:T(8,128)}, f32[128,768]{1,0:T(8,128)S(1)}, u32[]{:S(2)}, u32[]{:S(2)}) collective-permute-start(f32[128,768]{1,0:T(8,128)} %param.5), channel_id=1, source_target_pairs={{0,1},{1,0},{2,3},{3,2},{4,5},{5,4},{6,7},{7,6},{8,9},{9,8},{10,11... | collective-permute-start | bytes 1179656 | tf_op jit(solution)/shard_map/ppermute | solution.py:20
  7.4 12.6 %collective-permute-start.4 = (f32[128]{0:T(128)}, f32[128]{0:T(128)S(1)}, u32[]{:S(2)}, u32[]{:S(2)}) collective-permute-start(f32[128]{0:T(128)} %param.9), channel_id=1, source_target_pairs={{0,1},{1,0},{2,3},{3,2},{4,5},{5,4},{6,7},{7,6},{8,9},{9,8},{10,11... | collective-permute-start | bytes 1544 | tf_op jit(solution)/shard_map/ppermute | solution.py:20
  10.8 0.7 %copy-start.2 = (f32[128]{0:T(128)S(1)}, f32[128]{0:T(128)}, u32[]{:S(2)}) copy-start(f32[128]{0:T(128)} %param.9) | copy-start | bytes 1540
  18.8 7.3 %collective-permute-start.3 = (f32[128]{0:T(128)S(1)}, f32[128]{0:T(128)S(1)}, u32[]{:S(2)}, u32[]{:S(2)}) collective-permute-start(f32[128]{0:T(128)S(1)} %add_add_fusion), channel_id=1, source_target_pairs={{0,1},{1,0},{2,3},{3,2},{4,5},{5,4},{6,7},{7,6},{8,9},{9,8},{10,11... | collective-permute-start | bytes 1544 | tf_op jit(solution)/shard_map/ppermute | solution.py:20
  21.3 9.6 %collective-permute-start.5 = (f32[128,768]{1,0:T(8,128)S(1)}, f32[128,768]{1,0:T(8,128)S(1)}, u32[]{:S(2)}, u32[]{:S(2)}) collective-permute-start(f32[128,768]{1,0:T(8,128)S(1)} %fusion.1), channel_id=1, source_target_pairs={{0,1},{1,0},{2,3},{3,2},{4,5},{5,4},{6,7},{7,6},{8,9},{9,8},{10,11... | collective-permute-start | bytes 1179656 | tf_op jit(solution)/shard_map/ppermute | solution.py:20
  22.8 11.5 %collective-permute-start.7 = (f32[128,768]{1,0:T(8,128)S(1)}, f32[128,768]{1,0:T(8,128)S(1)}, u32[]{:S(2)}, u32[]{:S(2)}) collective-permute-start(f32[128,768]{1,0:T(8,128)S(1)} %convolution_add_fusion), channel_id=1, source_target_pairs={{2,4},{6,8},{10,12},{14,16},{18,20},{22,24},{26,28},{30,0},{4,2},{... | collective-permute-start | bytes 1179656 | tf_op jit(solution)/shard_map/ppermute | solution.py:15
  24.1 10.2 %collective-permute-start.6 = (f32[128,768]{1,0:T(8,128)S(1)}, f32[128,768]{1,0:T(8,128)S(1)}, u32[]{:S(2)}, u32[]{:S(2)}) collective-permute-start(f32[128,768]{1,0:T(8,128)S(1)} %convolution_add_fusion.1), channel_id=1, source_target_pairs={{0,2},{4,6},{8,10},{12,14},{16,18},{20,22},{24,26},{28,30},{2,0},{... | collective-permute-start | bytes 1179656 | tf_op jit(solution)/shard_map/ppermute | solution.py:15

commit v2 on v1

v2 whole, which is shorter than its diff:
```python
import functools

import jax
import jax.numpy as jnp
from jax import lax
from jax.experimental import pallas as pl
from jax.experimental.pallas import tpu as pltpu
from jax.sharding import PartitionSpec as P

BF = jnp.bfloat16
F32 = jnp.float32
VMEM = pl.BlockSpec(memory_space=pltpu.VMEM)
SMEM = pl.BlockSpec(memory_space=pltpu.SMEM)


def swapped(x, axis, near):
    length = lax.axis_size(axis)
    if near:
        pairs = [(i, i + 1) for i in range(0, length, 2)]
    else:
        pairs = [(i, (i + 1) % length) for i in range(1, length, 2)]
    return lax.ppermute(x, axis, pairs + [(b, a) for (a, b) in pairs])


def shifted(x, axis, by):
    length = lax.axis_size(axis)
    return lax.ppermute(x, axis, [(i, (i + by) % length) for i in range(length)])


def unit_of(raw):
    return raw * lax.rsqrt(jnp.sum(raw * raw, axis=1, keepdims=True) + 1e-06)


def split(v):
    high = v.astype(BF)
    return high, (v - high.astype(F32)).astype(BF)


def dot3(a, b, dims):
    def one(p, q):
        return lax.dot_general(p, q, (dims, ((), ())), preferred_element_type=F32)

    return one(a[0], b[0]) + (one(a[0], b[1]) + one(a[1], b[0]))


def scores(texts, images, temper, bias):
    return temper * dot3(texts, images, ((1,), (1,))) + bias


def terms(signed):
    small = jnp.exp(-jnp.abs(signed))
    loss = jnp.maximum(signed, 0.0) + jnp.log1p(small)
    gate = jnp.where(signed >= 0.0, 1.0, small) / (1.0 + small)
    return loss, gate


def slopes(texts, images, temper, bias, weight, diagonal=None):
    signed = scores(texts, images, temper, bias)
    if diagonal is not None:
        signed = jnp.where(diagonal, -signed, signed)
    loss, gate = terms(signed)
    slope = gate * weight
    if diagonal is not None:
        slope = jnp.where(diagonal, -slope, slope)
    return jnp.sum(loss, axis=0, keepdims=True), split(slope)


def joined(*pairs):
    return tuple(jnp.concatenate(p, axis=0) for p in zip(*pairs))


def part(pair, low, high):
    return pair[0][low:high], pair[1][low:high]


ON_ROWS = ((1,), (0,))
ON_COLS = ((0,), (0,))


def first_body(lt, bi, x_ref, y_ref, near_ref, w_ref, xs_ref, ys_ref, gx_ref, gy_ref, sum_ref):
    temper = jnp.exp(jnp.full((1, 1), lt[0], F32))
    bias = bi[0]
    count = x_ref.shape[0]
    weight = w_ref[...] * temper
    xs = split(unit_of(x_ref[...]))
    xs_ref[0], xs_ref[1] = xs
    own = split(unit_of(y_ref[...]))
    near = split(unit_of(near_ref[...]))
    ys = joined(own, near)
    ys_ref[0], ys_ref[1] = ys
    rows = lax.broadcasted_iota(jnp.int32, (2 * count, count), 0)
    cols = lax.broadcasted_iota(jnp.int32, (2 * count, count), 1)
    sums, slope = slopes(ys, xs, temper, bias, weight, rows == cols)
    sum_ref[...] = sums
    gx_ref[...] = dot3(slope, ys, ON_COLS)
    gy_ref[...] = dot3(slope, xs, ON_ROWS)


def second_body(others, lt, bi, *refs):
    raw_refs, refs = refs[:others], refs[others:]
    w_refs, refs = refs[: others + 1], refs[others + 1 :]
    far_ref, xs_ref, ys_ref, sum_in, refs = *refs[:4], refs[4:]
    gfar_ref, refs = refs[0], refs[1:]
    gp_refs, refs = refs[:others], refs[others:]
    sump_refs, refs = refs[:others], refs[others:]
    sum_ref, px_ref, ps_ref, fars_ref, fs_ref = refs
    temper = jnp.exp(jnp.full((1, 1), lt[0], F32))
    bias = bi[0]
    count = far_ref.shape[0]
    xs = (xs_ref[0], xs_ref[1])
    far = split(unit_of(far_ref[...]))
    fars_ref[0], fars_ref[1] = far
    ys = joined((ys_ref[0], ys_ref[1]), far)
    sums, slope = slopes(far, xs, temper, bias, w_refs[0][...] * temper)
    sum_ref[...] = sum_in[...] + sums
    fs_ref[0], fs_ref[1] = slope
    g_far = dot3(slope, xs, ON_ROWS)
    for s in range(others):
        xp = split(unit_of(raw_refs[s][...]))
        px_ref[s, 0], px_ref[s, 1] = xp
        sums, slope = slopes(ys, xp, temper, bias, w_refs[s + 1][...] * temper)
        sump_refs[s][...] = sums
        gp_refs[s][...] = dot3(slope, ys, ON_COLS)
        g_far = g_far + dot3(part(slope, 2 * count, 3 * count), xp, ON_ROWS)
        ps_ref[s, 0], ps_ref[s, 1] = part(slope, 0, 2 * count)
    gfar_ref[...] = g_far


def third_body(others, gx_in, gy_in, px_ref, ps_ref, fars_ref, fs_ref, gx_ref, gown_ref, gnear_ref):
    count = gx_in.shape[0]
    gy = gy_in[...]
    for s in range(others):
        gy = gy + dot3((ps_ref[s, 0], ps_ref[s, 1]), (px_ref[s, 0], px_ref[s, 1]), ON_ROWS)
    gown_ref[...] = gy[:count]
    gnear_ref[...] = gy[count:]
    gx_ref[...] = gx_in[...] + dot3((fs_ref[0], fs_ref[1]), (fars_ref[0], fars_ref[1]), ON_COLS)


def last_body(raw_ref, *refs):
    raw = raw_ref[...]
    grad = refs[0][...]
    for r in refs[1:-1]:
        grad = grad + r[...]
    scale = lax.rsqrt(jnp.sum(raw * raw, axis=1, keepdims=True) + 1e-06)
    unit = raw * scale
    refs[-1][...] = scale * (grad - unit * jnp.sum(unit * grad, axis=1, keepdims=True))


def shape(*dims, kind=F32):
    return jax.ShapeDtypeStruct(dims, kind)


def call(body, outs, count_in, scalars=0, final=False):
    run = pl.pallas_call(
        body,
        out_shape=outs if final else [pltpu.VMEM(o.shape, o.dtype) for o in outs],
        in_specs=[SMEM] * scalars + [VMEM] * count_in,
        out_specs=jax.tree.map(lambda _: VMEM, outs),
        compiler_params=pltpu.CompilerParams(vmem_limit_bytes=16 * 1024 * 1024),
    )

    def go(*args):
        held = [pltpu.with_memory_space_constraint(a, pltpu.VMEM) for a in args[scalars:]]
        return run(*args[:scalars], *held)

    return go


def shards(images, texts, log_temp, bias, row_weight):
    members = lax.axis_size("grp")
    others = members - 1
    count, width = images.shape
    weight = row_weight.reshape(1, count)
    far = swapped(texts, "blk", False)
    near = swapped(texts, "blk", True)
    raws = [shifted(images, "grp", -s) for s in range(1, members)]
    weights = [weight] + [shifted(weight, "grp", -s) for s in range(1, members)]
    full = shape(count, width)
    line = shape(1, count)
    xs, ys, gx, gy, sums = call(
        first_body,
        [
            shape(2, count, width, kind=BF),
            shape(2, 2 * count, width, kind=BF),
            full,
            shape(2 * count, width),
            line,
        ],
        4,
        2,
    )(log_temp, bias, images, texts, near, weight)
    outs = call(
        functools.partial(second_body, others),
        [full]
        + [full] * others
        + [line] * others
        + [
            line,
            shape(others, 2, count, width, kind=BF),
            shape(others, 2, 2 * count, count, kind=BF),
            shape(2, count, width, kind=BF),
            shape(2, count, count, kind=BF),
        ],
        2 * others + 5,
        2,
    )(log_temp, bias, *raws, *weights, far, xs, ys, sums)
    g_far, outs = outs[0], outs[1:]
    g_others, outs = outs[:others], outs[others:]
    s_others, outs = outs[:others], outs[others:]
    sums, px, ps, fars, fs = outs
    back_x = [shifted(g_others[s - 1], "grp", s) for s in range(1, members)]
    back_far = swapped(g_far, "blk", False)
    gx, g_own, g_near = call(functools.partial(third_body, others), [full, full, full], 6)(
        gx, gy, px, ps, fars, fs
    )
    back_near = swapped(g_near, "blk", True)
    for s in range(1, members):
        sums = sums + shifted(s_others[s - 1], "grp", s)
    row_loss = (sums / (3 * members * count)).reshape(count)
    grad_x = call(last_body, full, 2 + others, final=True)(images, gx, *back_x)
    grad_y = call(last_body, full, 4, final=True)(texts, g_own, back_near, back_far)
    return (row_loss, grad_x, grad_y)


def solution(mesh):
    placed = (P(("blk", "grp"), None), P(("blk", "grp"), None), P(), P(), P(("blk", "grp")))
    return jax.shard_map(
        shards,
        mesh=mesh,
        in_specs=placed,
        out_specs=(P(("blk", "grp")), P(("blk", "grp"), None), P(("blk", "grp"), None)),
        check_vma=False,
    )
```

time: 35.9 us -> 31.3 us (0.87)
  matrix products: 7.74 us -> 0 us
  Pallas kernels: 0 us -> 6.81 us
  other arithmetic: 3.88 us -> 0.51 us
  starting transfers between devices: 10.2 us -> 7.93 us
  local copies, waits for them, and re-layouts: 0.66 us -> 2 us
  waiting for transfers between devices: 11.1 us -> 11.8 us
    dot_general x18 -> x0, matrix products: 7.74 us -> none  [the longest x6 2.8 us: tile_terms(): jnp.einsum('id,jd->ij', left, right, precision=HIGH)]
    pallas_call x0 -> x5, Pallas kernels: none -> 6.81 us  [go(): return run(*args[:scalars], *held)]
    ppermute x4, starting transfers between devices: 7.11 us -> 3.71 us  [swapped(): return lax.ppermute(x, axis, pairs + [(b, a) for a, b in pairs])]
    mul x2 -> x0, other arithmetic: 1.79 us -> none  [unnormed(): return scale * (grad - unit * jnp.sum(unit * grad, axis=1, keepdims=True))]
    reduce_sum x5 -> x0, other arithmetic: 1.54 us -> none  [normed(): scale = lax.rsqrt(jnp.sum(values * values, axis=1, keepdims=True) + 1e-06)]
    ppermute x4, waiting for transfers between devices: 7.74 us -> 9.25 us  [shifted(): lax.ppermute(x, axis, [(i, (i + by) % length) for i in range(length)])]
    unnamed x6 -> x10, local copies, waits for them, and re-layouts: 0.66 us -> 2 us
    ppermute x4, starting transfers between devices: 3.06 us -> 4.22 us  [shifted(): lax.ppermute(x, axis, [(i, (i + by) % length) for i in range(length)])]
  transfers between devices with their start and end apart: 8 -> 8, of which waited for: 4 -> 4; matrix products, arithmetic and copies ran while one was open for 29% -> 2% of each run, Pallas kernels for 0% -> 11%
where the time goes in v2:
time: 31.3 us; the launch traced here: 31.1 us
  waiting for transfers between devices  11.8 us (38%)
  starting transfers between devices  7.93 us (25%)
  Pallas kernels  6.81 us (22%)
  local copies, waits for them, and re-layouts  2 us (6%)
  between operations  2 us (6%)
  other arithmetic  0.51 us (2%)
    ppermute x4, waiting for transfers between devices, shifted(): lax.ppermute(x, axis, [(i, (i + by) % length) for i in range(length)])  9.25 us
    pallas_call x5, Pallas kernels, go(): return run(*args[:scalars], *held)  6.81 us
    ppermute x4, starting transfers between devices, shifted(): lax.ppermute(x, axis, [(i, (i + by) % length) for i in range(length)])  4.22 us
    ppermute x4, starting transfers between devices, swapped(): return lax.ppermute(x, axis, pairs + [(b, a) for a, b in pairs])  3.71 us
    ppermute x4, waiting for transfers between devices, swapped(): return lax.ppermute(x, axis, pairs + [(b, a) for a, b in pairs])  2.56 us
    unnamed x10, local copies, waits for them, and re-layouts  2 us
  transfers between devices with their start and end apart: 8, of which 4 were waited for; matrix products, arithmetic and copies ran while one was open for 2% of the time, Pallas kernels for 11%

profile of v2, /device:TPU:1, one launch (start us, length us, event | category | flops | bytes accessed | tf_op | source)
XLA Modules:
  0.0 31.1 jit_solution(14571722048430516649)
XLA Ops:
  0.6 0.0 copy-start.4
  0.6 0.1 collective-permute-start.3
  0.7 2.7 %collective-permute-start = (f32[128,768]{1,0:T(8,128)}, f32[128,768]{1,0:T(8,128)S(1)}, u32[]{:S(2)}, u32[]{:S(2)}) collective-permute-start(f32[128,768]{1,0:T(8,128)} %raw_ref.2), channel_id=1, source_target_pairs={{0,1},{1,0},{2,3},{3,2},{4,5},{5,4},{6,7},{7,6},{8,9},{9,8},{10,11... | collective-permute-start | bytes 1179656 | tf_op jit(solution)/shard_map/ppermute | solution.py:27
  3.4 1.5 %collective-permute-start.2 = (f32[128,768]{1,0:T(8,128)}, f32[128,768]{1,0:T(8,128)S(1)}, u32[]{:S(2)}, u32[]{:S(2)}) collective-permute-start(f32[128,768]{1,0:T(8,128)} %raw_ref.3), channel_id=1, source_target_pairs={{2,4},{6,8},{10,12},{14,16},{18,20},{22,24},{26,28},{30,0},{4,2},{... | collective-permute-start | bytes 1179656 | tf_op jit(solution)/shard_map/ppermute | solution.py:22
  4.9 0.0 copy-done.4
  4.9 0.3 collective-permute-start.1
  6.5 0.0 collective-permute-done.3.near_ref
  6.5 0.0 copy-start
  6.5 1.0 %copy-done = f32[128,768]{1,0:T(8,128)S(1)} copy-done((f32[128,768]{1,0:T(8,128)S(1)}, f32[128,768]{1,0:T(8,128)}, u32[]{:S(2)}) %copy-start) | copy-done | bytes 393240
  7.5 0.0 copy-start.2
  7.5 1.0 %copy-done.2 = f32[128,768]{1,0:T(8,128)S(1)} copy-done((f32[128,768]{1,0:T(8,128)S(1)}, f32[128,768]{1,0:T(8,128)}, u32[]{:S(2)}) %copy-start.2) | copy-done | bytes 393240
  8.5 1.9 %shard_map.76 = (bf16[2,128,768]{2,1,0:T(8,128)(2,1)S(1)}, bf16[2,256,768]{2,1,0:T(8,128)(2,1)S(1)}, f32[128,768]{1,0:T(8,128)S(1)}, f32[256,768]{1,0:T(8,128)S(1)}, f32[1,128]{1,0:T(1,128)S(1)}) custom-call(f32[1]{0:T(128)S(6)} %copy.8.lt, f32[1]{0:T(128)S(6)} %copy.9.bi, f32[128,768]{1,0:T(8,128)S(1)} %copy-done, f32[128,768]{1,0:T(8,128)S(1)} %copy-done.2, ...), custom_call_target="tpu_custom_call" | custom-call | tf_op jit(solution)/shard_map/pallas_call | solution.py:164
  10.3 2.7 %collective-permute-done.1.refs_2_ = f32[1,128]{1,0:T(1,128)S(1)} collective-permute-done((f32[1,128]{1,0:T(1,128)S(1)}, f32[1,128]{1,0:T(1,128)S(1)}, u32[]{:S(2)}, u32[]{:S(2)}) %collective-permute-start.1) | collective-permute-done | bytes 544 | tf_op jit(solution)/shard_map/ppermute | solution.py:27
  13.0 0.0 collective-permute-done.refs_0_
  13.0 2.0 %collective-permute-done.2.refs_3_ = f32[128,768]{1,0:T(8,128)S(1)} collective-permute-done((f32[128,768]{1,0:T(8,128)}, f32[128,768]{1,0:T(8,128)S(1)}, u32[]{:S(2)}, u32[]{:S(2)}) %collective-permute-start.2) | collective-permute-done | bytes 393248 | tf_op jit(solution)/shard_map/ppermute | solution.py:22
  15.0 2.4 %shard_map.77 = (f32[128,768]{1,0:T(8,128)S(1)}, f32[128,768]{1,0:T(8,128)S(1)}, f32[1,128]{1,0:T(1,128)S(1)}, f32[1,128]{1,0:T(1,128)S(1)}, bf16[1,2,128,768]{3...) custom-call(f32[1]{0:T(128)S(6)} %copy.8.lt, ...), custom_call_target="tpu_custom_call" | custom-call | tf_op jit(solution)/shard_map/pallas_call | solution.py:164
  17.4 0.1 collective-permute-start.5
  17.5 0.0 copy-start.1
  17.5 0.6 %shard_map.78 = (f32[128,768]{1,0:T(8,128)S(1)}, f32[128,768]{1,0:T(8,128)S(1)}, f32[128,768]{1,0:T(8,128)S(1)}) custom-call(f32[128,768]{1,0:T(8,128)S(1)} %get-tuple-element.24.gx_in, f32[256,768]{1,0:T(8,128)S(1)} %get-tuple-element.25.gy_in, bf16[1,2,128,768]{3,2,1,0:T(8,128)(2,1)S(1)} %get-tuple-element.26.px_ref, ...), custom_call_target="tpu_custom_call" | custom-call | tf_op jit(solution)/shard_map/pallas_call | solution.py:164
  18.2 0.5 %collective-permute-start.6 = (f32[128,768]{1,0:T(8,128)S(1)}, f32[128,768]{1,0:T(8,128)S(1)}, u32[]{:S(2)}, u32[]{:S(2)}) collective-permute-start(f32[128,768]{1,0:T(8,128)S(1)} %get-tuple-element.33), channel_id=1, source_target_pairs={{0,2},{4,6},{8,10},{12,14},{16,18},{20,22},{24,26},{28,30},{2,0},{... | collective-permute-start | bytes 1179656 | tf_op jit(solution)/shard_map/ppermute | solution.py:22
  18.7 1.6 %collective-permute-start.7 = (f32[128,768]{1,0:T(8,128)S(1)}, f32[128,768]{1,0:T(8,128)S(1)}, u32[]{:S(2)}, u32[]{:S(2)}) collective-permute-start(f32[128,768]{1,0:T(8,128)S(1)} %get-tuple-element.34), channel_id=1, source_target_pairs={{2,4},{6,8},{10,12},{14,16},{18,20},{22,24},{26,28},{30,0},{4,2},{... | collective-permute-start | bytes 1179656 | tf_op jit(solution)/shard_map/ppermute | solution.py:22
  20.3 1.2 %collective-permute-start.4 = (f32[1,128]{1,0:T(1,128)S(1)}, f32[1,128]{1,0:T(1,128)S(1)}, u32[]{:S(2)}, u32[]{:S(2)}) collective-permute-start(f32[1,128]{1,0:T(1,128)S(1)} %get-tuple-element.23), channel_id=1, source_target_pairs={{0,1},{1,0},{2,3},{3,2},{4,5},{5,4},{6,7},{7,6},{8,9},{9,8},{10,11... | collective-permute-start | bytes 1544 | tf_op jit(solution)/shard_map/ppermute | solution.py:27
  21.5 6.6 %collective-permute-done.4 = f32[1,128]{1,0:T(1,128)S(1)} collective-permute-done((f32[1,128]{1,0:T(1,128)S(1)}, f32[1,128]{1,0:T(1,128)S(1)}, u32[]{:S(2)}, u32[]{:S(2)}) %collective-permute-start.4) | collective-permute-done | bytes 544 | tf_op jit(solution)/shard_map/ppermute | solution.py:27
  28.1 0.5 %multiply_bitcast_fusion = f32[128]{0:T(128)} fusion(f32[1,128]{1,0:T(1,128)S(1)} %get-tuple-element.22, f32[1,128]{1,0:T(1,128)S(1)} %collective-permute-done.4), kind=kLoop, calls=%fused_computation | loop fusion | flops 256 | bytes 1536 | tf_op jit(solution)/shard_map/reshape | solution.py:219
  28.6 0.0 collective-permute-done.5.refs_1_
  28.6 0.0 copy-done.1
  28.6 0.0 copy-start.3
  28.6 1.0 %shard_map.79 = f32[128,768]{1,0:T(8,128)} custom-call(f32[128,768]{1,0:T(8,128)S(1)} %copy-done.1, f32[128,768]{1,0:T(8,128)S(1)} %get-tuple-element.30.refs_0_, f32[128,768]{1,0:T(8,128)S(1)} %collective-permute-done.5.refs_1_), custom_call_target="tpu_custom_call" | custom-call | tf_op jit(solution)/shard_map/pallas_call | solution.py:164
  29.5 0.0 collective-permute-done.6.refs_1_
  29.5 0.6 %collective-permute-done.7.refs_2_ = f32[128,768]{1,0:T(8,128)S(1)} collective-permute-done((f32[128,768]{1,0:T(8,128)S(1)}, f32[128,768]{1,0:T(8,128)S(1)}, u32[]{:S(2)}, u32[]{:S(2)}) %collective-permute-start.7) | collective-permute-done | bytes 393248 | tf_op jit(solution)/shard_map/ppermute | solution.py:22
  30.1 0.0 copy-done.3
  30.1 1.0 %shard_map.80 = f32[128,768]{1,0:T(8,128)} custom-call(f32[128,768]{1,0:T(8,128)S(1)} %copy-done.3, f32[128,768]{1,0:T(8,128)S(1)} %get-tuple-element.32.refs_0_, f32[128,768]{1,0:T(8,128)S(1)} %collective-permute-done.6.refs_1_, f32[128,768]{1,0:T(8,128)S(1)} %collective-permute-done.7.refs_2_), custom_call_target="tpu_custom_call" | custom-call | tf_op jit(solution)/shard_map/pallas_call | solution.py:164
Async XLA Ops:
  0.6 4.3 %copy-start.4 = (f32[128]{0:T(128)S(1)}, f32[128]{0:T(128)}, u32[]{:S(2)}) copy-start(f32[128]{0:T(128)} %param.9) | copy-start | bytes 1540
  0.6 5.8 %collective-permute-start.3 = (f32[128,768]{1,0:T(8,128)}, f32[128,768]{1,0:T(8,128)S(1)}, u32[]{:S(2)}, u32[]{:S(2)}) collective-permute-start(f32[128,768]{1,0:T(8,128)} %raw_ref.3), channel_id=1, source_target_pairs={{0,2},{4,6},{8,10},{12,14},{16,18},{20,22},{24,26},{28,30},{2,0},{... | collective-permute-start | bytes 1179656 | tf_op jit(solution)/shard_map/ppermute | solution.py:22
  0.7 12.3 %collective-permute-start = (f32[128,768]{1,0:T(8,128)}, f32[128,768]{1,0:T(8,128)S(1)}, u32[]{:S(2)}, u32[]{:S(2)}) collective-permute-start(f32[128,768]{1,0:T(8,128)} %raw_ref.2), channel_id=1, source_target_pairs={{0,1},{1,0},{2,3},{3,2},{4,5},{5,4},{6,7},{7,6},{8,9},{9,8},{10,11... | collective-permute-start | bytes 1179656 | tf_op jit(solution)/shard_map/ppermute | solution.py:27
  3.4 11.6 %collective-permute-start.2 = (f32[128,768]{1,0:T(8,128)}, f32[128,768]{1,0:T(8,128)S(1)}, u32[]{:S(2)}, u32[]{:S(2)}) collective-permute-start(f32[128,768]{1,0:T(8,128)} %raw_ref.3), channel_id=1, source_target_pairs={{2,4},{6,8},{10,12},{14,16},{18,20},{22,24},{26,28},{30,0},{4,2},{... | collective-permute-start | bytes 1179656 | tf_op jit(solution)/shard_map/ppermute | solution.py:22
  4.9 8.1 %collective-permute-start.1 = (f32[1,128]{1,0:T(1,128)S(1)}, f32[1,128]{1,0:T(1,128)S(1)}, u32[]{:S(2)}, u32[]{:S(2)}) collective-permute-start(f32[1,128]{1,0:T(1,128)S(1)} %bitcast.3), channel_id=1, source_target_pairs={{0,1},{1,0},{2,3},{3,2},{4,5},{5,4},{6,7},{7,6},{8,9},{9,8},{10,11... | collective-permute-start | bytes 1544 | tf_op jit(solution)/shard_map/ppermute | solution.py:27
  6.5 1.0 %copy-start = (f32[128,768]{1,0:T(8,128)S(1)}, f32[128,768]{1,0:T(8,128)}, u32[]{:S(2)}) copy-start(f32[128,768]{1,0:T(8,128)} %raw_ref.2) | copy-start | bytes 1179652
  7.5 1.0 %copy-start.2 = (f32[128,768]{1,0:T(8,128)S(1)}, f32[128,768]{1,0:T(8,128)}, u32[]{:S(2)}) copy-start(f32[128,768]{1,0:T(8,128)} %raw_ref.3) | copy-start | bytes 1179652
  17.4 11.1 %collective-permute-start.5 = (f32[128,768]{1,0:T(8,128)S(1)}, f32[128,768]{1,0:T(8,128)S(1)}, u32[]{:S(2)}, u32[]{:S(2)}) collective-permute-start(f32[128,768]{1,0:T(8,128)S(1)} %get-tuple-element.31), channel_id=1, source_target_pairs={{0,1},{1,0},{2,3},{3,2},{4,5},{5,4},{6,7},{7,6},{8,9},{9,8},{10,11... | collective-permute-start | bytes 1179656 | tf_op jit(solution)/shard_map/ppermute | solution.py:27
  17.5 11.1 %copy-start.1 = (f32[128,768]{1,0:T(8,128)S(1)}, f32[128,768]{1,0:T(8,128)}, u32[]{:S(2)}) copy-start(f32[128,768]{1,0:T(8,128)} %raw_ref.2) | copy-start | bytes 1179652
  18.2 11.4 %collective-permute-start.6 = (f32[128,768]{1,0:T(8,128)S(1)}, f32[128,768]{1,0:T(8,128)S(1)}, u32[]{:S(2)}, u32[]{:S(2)}) collective-permute-start(f32[128,768]{1,0:T(8,128)S(1)} %get-tuple-element.33), channel_id=1, source_target_pairs={{0,2},{4,6},{8,10},{12,14},{16,18},{20,22},{24,26},{28,30},{2,0},{... | collective-permute-start | bytes 1179656 | tf_op jit(solution)/shard_map/ppermute | solution.py:22
  18.7 11.4 %collective-permute-start.7 = (f32[128,768]{1,0:T(8,128)S(1)}, f32[128,768]{1,0:T(8,128)S(1)}, u32[]{:S(2)}, u32[]{:S(2)}) collective-permute-start(f32[128,768]{1,0:T(8,128)S(1)} %get-tuple-element.34), channel_id=1, source_target_pairs={{2,4},{6,8},{10,12},{14,16},{18,20},{22,24},{26,28},{30,0},{4,2},{... | collective-permute-start | bytes 1179656 | tf_op jit(solution)/shard_map/ppermute | solution.py:22
  20.3 7.8 %collective-permute-start.4 = (f32[1,128]{1,0:T(1,128)S(1)}, f32[1,128]{1,0:T(1,128)S(1)}, u32[]{:S(2)}, u32[]{:S(2)}) collective-permute-start(f32[1,128]{1,0:T(1,128)S(1)} %get-tuple-element.23), channel_id=1, source_target_pairs={{0,1},{1,0},{2,3},{3,2},{4,5},{5,4},{6,7},{7,6},{8,9},{9,8},{10,11... | collective-permute-start | bytes 1544 | tf_op jit(solution)/shard_map/ppermute | solution.py:27
  28.6 1.5 %copy-start.3 = (f32[128,768]{1,0:T(8,128)S(1)}, f32[128,768]{1,0:T(8,128)}, u32[]{:S(2)}) copy-start(f32[128,768]{1,0:T(8,128)} %raw_ref.3) | copy-start | bytes 1179652

commit v3 on v1

v3 whole, which is shorter than its diff:
```python
import functools

import jax
import jax.numpy as jnp
from jax import lax
from jax.experimental import pallas as pl
from jax.experimental.pallas import tpu as pltpu
from jax.sharding import PartitionSpec as P


BF = jnp.bfloat16
F32 = jnp.float32
VMEM = pl.BlockSpec(memory_space=pltpu.VMEM)
SMEM = pl.BlockSpec(memory_space=pltpu.SMEM)
ANY = pl.BlockSpec(memory_space=pl.ANY)
CHUNKS = 4
NT = ((1,), (1,))
NN = ((1,), (0,))


def swapped(x, axis, near):
    length = lax.axis_size(axis)
    if near:
        pairs = [(i, i + 1) for i in range(0, length, 2)]
    else:
        pairs = [(i, (i + 1) % length) for i in range(1, length, 2)]
    return lax.ppermute(x, axis, pairs + [(b, a) for (a, b) in pairs])


def shifted(x, axis, by):
    length = lax.axis_size(axis)
    return lax.ppermute(x, axis, [(i, (i + by) % length) for i in range(length)])


def unit_of(raw):
    return raw * lax.rsqrt(jnp.sum(raw * raw, axis=1, keepdims=True) + 1e-06)


def stacked(v):
    high = v.astype(BF)
    return jnp.concatenate([high, (v - high.astype(F32)).astype(BF)], axis=0)


def mm(a, b, dims):
    rows = a.shape[0] // 2
    deep = b.shape[0] // 2

    def one(p, q):
        return lax.dot_general(p, q, (dims, ((), ())), preferred_element_type=F32)

    both = one(a[...], b[:deep])
    return both[:rows] + (both[rows:] + one(a[:rows], b[deep:]))


def gated(z, weight, diagonal=None):
    signed = z if diagonal is None else jnp.where(diagonal, -z, z)
    small = jnp.exp(-jnp.abs(signed))
    loss = jnp.maximum(signed, 0.0) + jnp.log1p(small)
    slope = jnp.where(signed >= 0.0, 1.0, small) / (1.0 + small) * weight
    if diagonal is not None:
        slope = jnp.where(diagonal, -slope, slope)
    return jnp.sum(loss, axis=0, keepdims=True), slope


def temper_of(lt):
    return jnp.exp(jnp.full((1, 1), lt[0], F32))


def first_body(lt, bi, x_ref, y_ref, near_ref, w_ref, xs_ref, ys_ref, gx_ref, gy_ref, sum_ref):
    temper = temper_of(lt)
    count = x_ref.shape[0]
    xs_ref[...] = stacked(unit_of(x_ref[...]))
    ys = jnp.concatenate([unit_of(y_ref[...]), unit_of(near_ref[...])], axis=0)
    ys_ref[...] = stacked(ys)
    rows = lax.broadcasted_iota(jnp.int32, (2 * count, count), 0)
    cols = lax.broadcasted_iota(jnp.int32, (2 * count, count), 1)
    z = temper * mm(ys_ref, xs_ref, NT) + bi[0]
    sums, slope = gated(z, w_ref[...] * temper, rows == cols)
    sum_ref[...] = sums
    gx_ref[...] = mm(stacked(slope.T), ys_ref, NN)
    gy_ref[...] = mm(stacked(slope), xs_ref, NN)


def second_body(others, lt, bi, *refs):
    raw_refs, refs = refs[:others], refs[others:]
    w_refs, refs = refs[:others], refs[others:]
    ys_ref, gy_in, refs = refs[0], refs[1], refs[2:]
    px_refs, refs = refs[:others], refs[others:]
    gp_refs, refs = refs[:others], refs[others:]
    sump_refs, refs = refs[:others], refs[others:]
    gown_ref, gnear_ref = refs
    temper = temper_of(lt)
    count = raw_refs[0].shape[0]
    gy = gy_in[...]
    for s in range(others):
        px_refs[s][...] = stacked(unit_of(raw_refs[s][...]))
        z = temper * mm(ys_ref, px_refs[s], NT) + bi[0]
        sump_refs[s][...], slope = gated(z, w_refs[s][...] * temper)
        gp_refs[s][...] = mm(stacked(slope.T), ys_ref, NN)
        gy = gy + mm(stacked(slope), px_refs[s], NN)
    gown_ref[...] = gy[:count]
    gnear_ref[...] = gy[count:]


def third_body(others, lt, bi, *refs):
    members = others + 1
    far_ref, refs = refs[0], refs[1:]
    w_refs, refs = refs[:members], refs[members:]
    x_refs, refs = refs[:members], refs[members:]
    gp_in, refs = refs[:others], refs[others:]
    sum_in, refs = refs[:members], refs[members:]
    gfar_ref, refs = refs[0], refs[1:]
    gp_refs, refs = refs[:others], refs[others:]
    sum_refs, refs = refs[:members], refs[members:]
    fs_ref, slope_ref = refs
    temper = temper_of(lt)
    fs_ref[...] = stacked(unit_of(far_ref[...]))
    gfar = None
    for s in range(members):
        z = temper * mm(fs_ref, x_refs[s], NT) + bi[0]
        sums, slope = gated(z, w_refs[s][...] * temper)
        sum_refs[s][...] = sum_in[s][...] + sums
        g = mm(stacked(slope), x_refs[s], NN)
        gfar = g if gfar is None else gfar + g
        if s == 0:
            slope_ref[...] = stacked(slope.T)
        else:
            gp_refs[s - 1][...] = gp_in[s - 1][...] + mm(stacked(slope.T), fs_ref, NN)
    gfar_ref[...] = gfar


def fourth_body(gx_in, slope_ref, fs_ref, gx_ref):
    gx_ref[...] = gx_in[...] + mm(slope_ref, fs_ref, NN)


def last_body(terms, sums, pairs, raw_ref, *refs):
    grads, refs = refs[:terms], refs[terms:]
    lines, refs = refs[:sums], refs[sums:]
    out_ref, refs = refs[0], refs[1:]
    if sums:
        total = lines[0][...]
        for r in lines[1:]:
            total = total + r[...]
        refs[0][...] = total / pairs
        refs = refs[1:]
    held, sem = refs
    rows = raw_ref.shape[0] // CHUNKS
    copies = []
    for c in range(CHUNKS):
        here = pl.ds(c * rows, rows)
        raw = raw_ref[here, :]
        grad = grads[0][here, :]
        for r in grads[1:]:
            grad = grad + r[here, :]
        scale = lax.rsqrt(jnp.sum(raw * raw, axis=1, keepdims=True) + 1e-06)
        unit = raw * scale
        held[here, :] = scale * (grad - unit * jnp.sum(unit * grad, axis=1, keepdims=True))
        copies.append(pltpu.make_async_copy(held.at[here, :], out_ref.at[here, :], sem.at[c]))
        copies[-1].start()
    for copy in copies:
        copy.wait()


def shape(*dims, kind=F32):
    return jax.ShapeDtypeStruct(dims, kind)


PARAMS = pltpu.CompilerParams(vmem_limit_bytes=16 * 1024 * 1024)


def in_vmem(args):
    return [pltpu.with_memory_space_constraint(a, pltpu.VMEM) for a in args]


def call(body, outs, scalars, *args):
    return pl.pallas_call(
        body,
        out_shape=[pltpu.VMEM(o.shape, o.dtype) for o in outs],
        in_specs=[SMEM] * len(scalars) + [VMEM] * len(args),
        out_specs=[VMEM] * len(outs),
        compiler_params=PARAMS,
    )(*scalars, *in_vmem(args))


def finish(raw, grads, lines, pairs):
    like = jax.ShapeDtypeStruct(raw.shape, raw.dtype)
    line = shape(1, raw.shape[0])
    return pl.pallas_call(
        functools.partial(last_body, len(grads), len(lines), pairs),
        out_shape=[like, line] if lines else [like],
        in_specs=[VMEM] * (1 + len(grads) + len(lines)),
        out_specs=[ANY, VMEM] if lines else [ANY],
        scratch_shapes=[pltpu.VMEM(raw.shape, F32), pltpu.SemaphoreType.DMA((CHUNKS,))],
        compiler_params=PARAMS,
    )(*in_vmem([raw, *grads, *lines]))


def body(images, texts, log_temp, bias, row_weight):
    members = lax.axis_size("grp")
    others = members - 1
    count, width = images.shape
    weight = row_weight.reshape(1, count)
    scalars = (log_temp, bias)
    raws = [shifted(images, "grp", -s) for s in range(1, members)]
    far = swapped(texts, "blk", False)
    near = swapped(texts, "blk", True)
    weights = [weight] + [shifted(weight, "grp", -s) for s in range(1, members)]
    full = shape(count, width)
    line = shape(1, count)
    stack = shape(2 * count, width, kind=BF)
    xs, ys, gx, gy, sums = call(
        first_body,
        [stack, shape(4 * count, width, kind=BF), full, shape(2 * count, width), line],
        scalars,
        images,
        texts,
        near,
        weight,
    )
    outs = call(
        functools.partial(second_body, others),
        [stack] * others + [full] * others + [line] * others + [full, full],
        scalars,
        *raws,
        *weights[1:],
        ys,
        gy,
    )
    px, outs = outs[:others], outs[others:]
    gp, outs = outs[:others], outs[others:]
    sump, (g_own, g_near) = outs[:others], outs[others:]
    back_near = swapped(g_near, "blk", True)
    outs = call(
        functools.partial(third_body, others),
        [full]
        + [full] * others
        + [line] * members
        + [stack, shape(2 * count, count, kind=BF)],
        scalars,
        far,
        *weights,
        xs,
        *px,
        *gp,
        sums,
        *sump,
    )
    g_far, outs = outs[0], outs[1:]
    gp, outs = outs[:others], outs[others:]
    sums, (fs, slope) = outs[:members], outs[members:]
    back_far = swapped(g_far, "blk", False)
    back_x = [shifted(gp[s - 1], "grp", s) for s in range(1, members)]
    back_sum = [shifted(sums[s], "grp", s) for s in range(1, members)]
    gx = call(fourth_body, [full], (), gx, slope, fs)[0]
    grad_x, row_loss = finish(images, [gx, *back_x], [sums[0], *back_sum], 3.0 * members * count)
    grad_y = finish(texts, [g_own, back_near, back_far], [], None)[0]
    return (row_loss.reshape(count), grad_x, grad_y)


def solution(mesh):
    placed = (P(("blk", "grp"), None), P(("blk", "grp"), None), P(), P(), P(("blk", "grp")))
    return jax.shard_map(
        body,
        mesh=mesh,
        in_specs=placed,
        out_specs=(P(("blk", "grp")), P(("blk", "grp"), None), P(("blk", "grp"), None)),
        check_vma=False,
    )
```

time: 35.9 us -> 34.6 us (0.964)
  the two profiles are of different devices: /device:TPU:1 before, /device:TPU:0 now
where the time goes in v3:
time: 34.6 us; the launch traced here: 34.3 us
  starting transfers between devices  13.9 us (40%)
  waiting for transfers between devices  8.31 us (24%)
  Pallas kernels  8.13 us (23%)
  between operations  2.02 us (6%)
  local copies, waits for them, and re-layouts  2 us (6%)
    ppermute x4, starting transfers between devices, swapped(): return lax.ppermute(x, axis, pairs + [(b, a) for a, b in pairs])  8.78 us
    pallas_call x4, Pallas kernels, call(): pl.pallas_call(body, out_shape=[pltpu.VMEM(o.shape, o.dtype) for o in out...  5.69 us
    ppermute x4, starting transfers between devices, shifted(): lax.ppermute(x, axis, [(i, (i + by) % length) for i in range(length)])  5.12 us
    ppermute x4, waiting for transfers between devices, shifted(): lax.ppermute(x, axis, [(i, (i + by) % length) for i in range(length)])  4.49 us
    ppermute x4, waiting for transfers between devices, swapped(): return lax.ppermute(x, axis, pairs + [(b, a) for a, b in pairs])  3.82 us
    pallas_call x2, Pallas kernels, finish(): pl.pallas_call(functools.partial(last_body, len(grads), len(lines), pairs...  2.43 us
    unnamed x10, local copies, waits for them, and re-layouts  2 us
  transfers between devices with their start and end apart: 8, of which 2 were waited for; matrix products, arithmetic and copies ran while one was open for 0% of the time, Pallas kernels for 15%

profile of v3, /device:TPU:0, one launch (start us, length us, event | category | flops | bytes accessed | tf_op | source)
XLA Modules:
  0.0 34.3 jit_solution(14278513326574278728)
XLA Ops:
  0.6 0.0 copy-start.4
  0.6 0.6 %collective-permute-start = (f32[128,768]{1,0:T(8,128)}, f32[128,768]{1,0:T(8,128)S(1)}, u32[]{:S(2)}, u32[]{:S(2)}) collective-permute-start(f32[128,768]{1,0:T(8,128)} %raw_ref.3), channel_id=1, source_target_pairs={{0,2},{4,6},{8,10},{12,14},{16,18},{20,22},{24,26},{28,30},{2,0},{... | collective-permute-start | bytes 1179656 | tf_op jit(solution)/shard_map/ppermute | solution.py:27
  1.2 2.6 %collective-permute-start.3 = (f32[128,768]{1,0:T(8,128)}, f32[128,768]{1,0:T(8,128)S(1)}, u32[]{:S(2)}, u32[]{:S(2)}) collective-permute-start(f32[128,768]{1,0:T(8,128)} %raw_ref.2), channel_id=1, source_target_pairs={{0,1},{1,0},{2,3},{3,2},{4,5},{5,4},{6,7},{7,6},{8,9},{9,8},{10,11... | collective-permute-start | bytes 1179656 | tf_op jit(solution)/shard_map/ppermute | solution.py:32
  3.8 4.3 %collective-permute-start.1 = (f32[128,768]{1,0:T(8,128)}, f32[128,768]{1,0:T(8,128)S(1)}, u32[]{:S(2)}, u32[]{:S(2)}) collective-permute-start(f32[128,768]{1,0:T(8,128)} %raw_ref.3), channel_id=1, source_target_pairs={{2,4},{6,8},{10,12},{14,16},{18,20},{22,24},{26,28},{30,0},{4,2},{... | collective-permute-start | bytes 1179656 | tf_op jit(solution)/shard_map/ppermute | solution.py:27
  8.1 0.0 copy-done.4
  8.1 0.5 %collective-permute-start.2 = (f32[1,128]{1,0:T(1,128)S(1)}, f32[1,128]{1,0:T(1,128)S(1)}, u32[]{:S(2)}, u32[]{:S(2)}) collective-permute-start(f32[1,128]{1,0:T(1,128)S(1)} %bitcast.2), channel_id=1, source_target_pairs={{0,1},{1,0},{2,3},{3,2},{4,5},{5,4},{6,7},{7,6},{8,9},{9,8},{10,11... | collective-permute-start | bytes 1544 | tf_op jit(solution)/shard_map/ppermute | solution.py:32
  9.9 0.0 collective-permute-done.near_ref
  9.9 0.0 copy-start
  9.9 1.0 %copy-done = f32[128,768]{1,0:T(8,128)S(1)} copy-done((f32[128,768]{1,0:T(8,128)S(1)}, f32[128,768]{1,0:T(8,128)}, u32[]{:S(2)}) %copy-start) | copy-done | bytes 393240
  10.9 0.0 copy-start.2
  10.9 1.0 %copy-done.2 = f32[128,768]{1,0:T(8,128)S(1)} copy-done((f32[128,768]{1,0:T(8,128)S(1)}, f32[128,768]{1,0:T(8,128)}, u32[]{:S(2)}) %copy-start.2) | copy-done | bytes 393240
  11.9 1.9 %shard_map.76 = (bf16[256,768]{1,0:T(8,128)(2,1)S(1)}, bf16[512,768]{1,0:T(8,128)(2,1)S(1)}, f32[128,768]{1,0:T(8,128)S(1)}, f32[256,768]{1,0:T(8,128)S(1)}, f32[1,128]{1,0:T(1,128)S(1)}) custom-call(f32[1]{0:T(128)S(6)} %copy.8.lt, f32[1]{0:T(128)S(6)} %copy.9.bi, f32[128,768]{1,0:T(8,128)S(1)} %copy-done, f32[128,768]{1,0:T(8,128)S(1)} %copy-done.2, ...), custom_call_target="tpu_custom_call" | custom-call | tf_op jit(solution)/shard_map/pallas_call | solution.py:176
  13.8 0.0 collective-permute-done.2.refs_1_.refs_2_
  13.8 0.0 collective-permute-done.3.refs_0_
  13.8 1.9 %shard_map.77 = (bf16[256,768]{1,0:T(8,128)(2,1)S(1)}, f32[128,768]{1,0:T(8,128)S(1)}, f32[1,128]{1,0:T(1,128)S(1)}, f32[128,768]{1,0:T(8,128)S(1)}, f32[128,768]{1,0:T(8,128)S(1)}) custom-call(f32[1]{0:T(128)S(6)} %copy.8.lt, f32[1]{0:T(128)S(6)} %copy.9.bi, f32[128,768]{1,0:T(8,128)S(1)} %collective-permute-done.3.refs_0_, ...), custom_call_target="tpu_custom_call" | custom-call | tf_op jit(solution)/shard_map/pallas_call | solution.py:176
  15.7 0.0 collective-permute-done.1.refs_0_
  15.7 1.6 %shard_map.78 = (f32[128,768]{1,0:T(8,128)S(1)}, f32[128,768]{1,0:T(8,128)S(1)}, f32[1,128]{1,0:T(1,128)S(1)}, f32[1,128]{1,0:T(1,128)S(1)}, bf16[256,768]{1,0:T(8,128)(2,1)S(1)}, /*index=5*/bf16[256,128]{1,0:T(8,128)(2,1)S(1)}) custom-call(f32[1]{0:T(128)S(6)} %copy.8.lt, f32[1]{0:T(128)S(6)} %copy.9.bi, f32[128,768]{1,0:T(8,128)S(1)} %collective-permute-done.1.refs_0_, ...), custom_call_target="tpu_custom_call" | custom-call | tf_op jit(solution)/shard_map/pallas_call | solution.py:176
  17.3 3.9 %collective-permute-start.7 = (f32[128,768]{1,0:T(8,128)S(1)}, f32[128,768]{1,0:T(8,128)S(1)}, u32[]{:S(2)}, u32[]{:S(2)}) collective-permute-start(f32[128,768]{1,0:T(8,128)S(1)} %get-tuple-element.38), channel_id=1, source_target_pairs={{2,4},{6,8},{10,12},{14,16},{18,20},{22,24},{26,28},{30,0},{4,2},{... | collective-permute-start | bytes 1179656 | tf_op jit(solution)/shard_map/ppermute | solution.py:27
  21.2 0.0 collective-permute-start.6
  21.3 1.5 %collective-permute-start.4 = (f32[128,768]{1,0:T(8,128)S(1)}, f32[128,768]{1,0:T(8,128)S(1)}, u32[]{:S(2)}, u32[]{:S(2)}) collective-permute-start(f32[128,768]{1,0:T(8,128)S(1)} %get-tuple-element.31), channel_id=1, source_target_pairs={{0,1},{1,0},{2,3},{3,2},{4,5},{5,4},{6,7},{7,6},{8,9},{9,8},{10,11... | collective-permute-start | bytes 1179656 | tf_op jit(solution)/shard_map/ppermute | solution.py:32
  22.7 0.5 %collective-permute-start.5 = (f32[1,128]{1,0:T(1,128)S(1)}, f32[1,128]{1,0:T(1,128)S(1)}, u32[]{:S(2)}, u32[]{:S(2)}) collective-permute-start(f32[1,128]{1,0:T(1,128)S(1)} %get-tuple-element.33), channel_id=1, source_target_pairs={{0,1},{1,0},{2,3},{3,2},{4,5},{5,4},{6,7},{7,6},{8,9},{9,8},{10,11... | collective-permute-start | bytes 1544 | tf_op jit(solution)/shard_map/ppermute | solution.py:32
  23.3 0.0 copy-start.3
  23.3 0.3 shard_map.79.refs_0_
  23.6 3.8 %collective-permute-done.7.refs_2_ = f32[128,768]{1,0:T(8,128)S(1)} collective-permute-done((f32[128,768]{1,0:T(8,128)S(1)}, f32[128,768]{1,0:T(8,128)S(1)}, u32[]{:S(2)}, u32[]{:S(2)}) %collective-permute-start.7) | collective-permute-done | bytes 393248 | tf_op jit(solution)/shard_map/ppermute | solution.py:27
  27.4 0.0 collective-permute-done.6.refs_1_
  27.4 0.0 copy-done.3
  27.4 0.0 copy-start.1
  27.4 1.0 %shard_map.81 = f32[128,768]{1,0:T(8,128)} custom-call(f32[128,768]{1,0:T(8,128)S(1)} %copy-done.3, f32[128,768]{1,0:T(8,128)S(1)} %get-tuple-element.36.refs_0_, f32[128,768]{1,0:T(8,128)S(1)} %collective-permute-done.6.refs_1_, f32[128,768]{1,0:T(8,128)S(1)} %collective-permute-done.7.refs_2_), custom_call_target="tpu_custom_call" | custom-call | tf_op jit(solution)/shard_map/pallas_call | solution.py:188
  28.4 4.5 %collective-permute-done.5.refs_3_ = f32[1,128]{1,0:T(1,128)S(1)} collective-permute-done((f32[1,128]{1,0:T(1,128)S(1)}, f32[1,128]{1,0:T(1,128)S(1)}, u32[]{:S(2)}, u32[]{:S(2)}) %collective-permute-start.5) | collective-permute-done | bytes 544 | tf_op jit(solution)/shard_map/ppermute | solution.py:32
  32.9 0.0 collective-permute-done.4.refs_1_
  32.9 0.0 copy-done.1
  32.9 1.5 %shard_map.80 = (f32[128,768]{1,0:T(8,128)}, f32[1,128]{1,0:T(1,128)}) custom-call(f32[128,768]{1,0:T(8,128)S(1)} %copy-done.1, f32[128,768]{1,0:T(8,128)S(1)} %shard_map.79.refs_0_, f32[128,768]{1,0:T(8,128)S(1)} %collective-permute-done.4.refs_1_, f32[1,128]{1,0:T(1,128)S(1)} %get-tuple-element.32.refs_2_, f32[1,128]{1,0:T(1,128)S(1)} %collective-permute-done.5.refs_3_), custom_call_target="tpu_custom_call" | custom-call | tf_op jit(solution)/shard_map/pallas_call | solution.py:188
Async XLA Ops:
  0.6 7.4 %copy-start.4 = (f32[128]{0:T(128)S(1)}, f32[128]{0:T(128)}, u32[]{:S(2)}) copy-start(f32[128]{0:T(128)} %param.9) | copy-start | bytes 1540
  0.6 9.3 %collective-permute-start = (f32[128,768]{1,0:T(8,128)}, f32[128,768]{1,0:T(8,128)S(1)}, u32[]{:S(2)}, u32[]{:S(2)}) collective-permute-start(f32[128,768]{1,0:T(8,128)} %raw_ref.3), channel_id=1, source_target_pairs={{0,2},{4,6},{8,10},{12,14},{16,18},{20,22},{24,26},{28,30},{2,0},{... | collective-permute-start | bytes 1179656 | tf_op jit(solution)/shard_map/ppermute | solution.py:27
  1.2 12.6 %collective-permute-start.3 = (f32[128,768]{1,0:T(8,128)}, f32[128,768]{1,0:T(8,128)S(1)}, u32[]{:S(2)}, u32[]{:S(2)}) collective-permute-start(f32[128,768]{1,0:T(8,128)} %raw_ref.2), channel_id=1, source_target_pairs={{0,1},{1,0},{2,3},{3,2},{4,5},{5,4},{6,7},{7,6},{8,9},{9,8},{10,11... | collective-permute-start | bytes 1179656 | tf_op jit(solution)/shard_map/ppermute | solution.py:32
  3.8 11.9 %collective-permute-start.1 = (f32[128,768]{1,0:T(8,128)}, f32[128,768]{1,0:T(8,128)S(1)}, u32[]{:S(2)}, u32[]{:S(2)}) collective-permute-start(f32[128,768]{1,0:T(8,128)} %raw_ref.3), channel_id=1, source_target_pairs={{2,4},{6,8},{10,12},{14,16},{18,20},{22,24},{26,28},{30,0},{4,2},{... | collective-permute-start | bytes 1179656 | tf_op jit(solution)/shard_map/ppermute | solution.py:27
  8.1 5.7 %collective-permute-start.2 = (f32[1,128]{1,0:T(1,128)S(1)}, f32[1,128]{1,0:T(1,128)S(1)}, u32[]{:S(2)}, u32[]{:S(2)}) collective-permute-start(f32[1,128]{1,0:T(1,128)S(1)} %bitcast.2), channel_id=1, source_target_pairs={{0,1},{1,0},{2,3},{3,2},{4,5},{5,4},{6,7},{7,6},{8,9},{9,8},{10,11... | collective-permute-start | bytes 1544 | tf_op jit(solution)/shard_map/ppermute | solution.py:32
  9.9 1.0 %copy-start = (f32[128,768]{1,0:T(8,128)S(1)}, f32[128,768]{1,0:T(8,128)}, u32[]{:S(2)}) copy-start(f32[128,768]{1,0:T(8,128)} %raw_ref.2) | copy-start | bytes 1179652
  10.9 1.0 %copy-start.2 = (f32[128,768]{1,0:T(8,128)S(1)}, f32[128,768]{1,0:T(8,128)}, u32[]{:S(2)}) copy-start(f32[128,768]{1,0:T(8,128)} %raw_ref.3) | copy-start | bytes 1179652
  17.3 10.1 %collective-permute-start.7 = (f32[128,768]{1,0:T(8,128)S(1)}, f32[128,768]{1,0:T(8,128)S(1)}, u32[]{:S(2)}, u32[]{:S(2)}) collective-permute-start(f32[128,768]{1,0:T(8,128)S(1)} %get-tuple-element.38), channel_id=1, source_target_pairs={{2,4},{6,8},{10,12},{14,16},{18,20},{22,24},{26,28},{30,0},{4,2},{... | collective-permute-start | bytes 1179656 | tf_op jit(solution)/shard_map/ppermute | solution.py:27
  21.2 6.2 %collective-permute-start.6 = (f32[128,768]{1,0:T(8,128)S(1)}, f32[128,768]{1,0:T(8,128)S(1)}, u32[]{:S(2)}, u32[]{:S(2)}) collective-permute-start(f32[128,768]{1,0:T(8,128)S(1)} %get-tuple-element.37), channel_id=1, source_target_pairs={{0,2},{4,6},{8,10},{12,14},{16,18},{20,22},{24,26},{28,30},{2,0},{... | collective-permute-start | bytes 1179656 | tf_op jit(solution)/shard_map/ppermute | solution.py:27
  21.3 11.6 %collective-permute-start.4 = (f32[128,768]{1,0:T(8,128)S(1)}, f32[128,768]{1,0:T(8,128)S(1)}, u32[]{:S(2)}, u32[]{:S(2)}) collective-permute-start(f32[128,768]{1,0:T(8,128)S(1)} %get-tuple-element.31), channel_id=1, source_target_pairs={{0,1},{1,0},{2,3},{3,2},{4,5},{5,4},{6,7},{7,6},{8,9},{9,8},{10,11... | collective-permute-start | bytes 1179656 | tf_op jit(solution)/shard_map/ppermute | solution.py:32
  22.7 10.1 %collective-permute-start.5 = (f32[1,128]{1,0:T(1,128)S(1)}, f32[1,128]{1,0:T(1,128)S(1)}, u32[]{:S(2)}, u32[]{:S(2)}) collective-permute-start(f32[1,128]{1,0:T(1,128)S(1)} %get-tuple-element.33), channel_id=1, source_target_pairs={{0,1},{1,0},{2,3},{3,2},{4,5},{5,4},{6,7},{7,6},{8,9},{9,8},{10,11... | collective-permute-start | bytes 1544 | tf_op jit(solution)/shard_map/ppermute | solution.py:32
  23.3 4.1 %copy-start.3 = (f32[128,768]{1,0:T(8,128)S(1)}, f32[128,768]{1,0:T(8,128)}, u32[]{:S(2)}) copy-start(f32[128,768]{1,0:T(8,128)} %raw_ref.3) | copy-start | bytes 1179652
  27.4 5.5 %copy-start.1 = (f32[128,768]{1,0:T(8,128)S(1)}, f32[128,768]{1,0:T(8,128)}, u32[]{:S(2)}) copy-start(f32[128,768]{1,0:T(8,128)} %raw_ref.2) | copy-start | bytes 1179652
